TPU v7x, 32 devices: a whole 2x2x4 slice. The times are simulated.
32 devices in a mesh: pairs: 2 (over x), band: 16 (over z, y, core).
Axes of the slice: x: 2, y: 2, z: 4, core: 2. Of those that a mesh axis runs over, the one named last changes fastest.
Arguments:
- query_tiles: bfloat16 [512, 256, 128], P(('pairs', 'band')), parts along dimension 0, may hold values from -52 to 52
- target: bfloat16 [512, 256, 128], P(('pairs', 'band')), parts along dimension 0, may hold values from -6 to 6
- tile_home: int32 [512], P('pairs'), parts along dimension 0, may hold values from 0 to 255, as said below
- candidates: int32 [512, 64], P(('pairs', 'band')), parts along dimension 0, may hold values from 0 to 255, as said below
- valid_mask: int32 [512, 64], P(('pairs', 'band')), parts along dimension 0, may hold values from 0 to 1, as said below
Outputs:
- matched: bfloat16 [512, 256, 128], P(('pairs', 'band')), parts along dimension 0
There are 2 independent parts, one for each index of `pairs`. A program takes and returns all parts, laid end to end along the dimension named above; each array names one. Nothing has to cross between parts.
Inputs may be any that keep to these rules, and one draw needn't show every extreme that they name: `tile_home`: a permutation of 0 to 255; target tile ids that agree modulo 16 are stored on the same device, storage row r lying on device r // 16. Ids in a row are distinct; the candidates of one device's query tiles all lie in one run of 128 consecutive ids taken modulo 256, and its first two query tiles together name every id of that run. `valid_mask`: the first entry of every row is 1.
All inputs are finite; a program needn't handle non-finite values.
Results may differ from a plain program's by a relative error of at most 0.0034.
Values may be sent and summed in bfloat16 or wider, within the bound.
No kernel may reach another device: no remote copies, remote signals or barrier semaphores. Data moves between devices by JAX's collectives and lax.ppermute only.
A program may use at most 128 MiB of HBM per device.

v0:
```python
import math
import jax
import jax.numpy as jnp
from jax import lax
from jax.sharding import PartitionSpec as P


def attend_tile(tile_query, tile_keys, keep_mask):
    per_tile = tile_keys.shape[0] // keep_mask.shape[0]
    scores = jnp.dot(tile_query, tile_keys.T, preferred_element_type=jnp.float32) * (
        1.0 / math.sqrt(tile_query.shape[1])
    )
    allowed = jnp.repeat(keep_mask > 0, per_tile)[None, :]
    scores = jnp.where(allowed, scores, -jnp.inf)
    peak = jnp.max(scores, axis=1, keepdims=True)
    raised = jnp.exp(scores - peak)
    totals = jnp.sum(raised, axis=1, keepdims=True)
    weights = (raised / totals).astype(jnp.bfloat16)
    return jnp.dot(weights, tile_keys, preferred_element_type=jnp.float32).astype(jnp.bfloat16)


def body(query_tiles, target, tile_home, candidates, valid_mask):
    channels = target.shape[2]
    stored_rows = tile_home[candidates]
    source = lax.all_gather(target, "band", axis=0, tiled=True)

    def one_tile(packed):
        tile_query, chosen, keep_mask = packed
        stored = source[chosen].reshape(-1, channels)
        return attend_tile(tile_query, stored, keep_mask)

    return lax.map(one_tile, (query_tiles, stored_rows, valid_mask))


def solution(mesh):
    in_specs = (
        P(("pairs", "band"), None, None),
        P(("pairs", "band"), None, None),
        P("pairs"),
        P(("pairs", "band"), None),
        P(("pairs", "band"), None),
    )
    out_specs = P(("pairs", "band"), None, None)
    return jax.shard_map(body, mesh=mesh, in_specs=in_specs, out_specs=out_specs, check_vma=False)
```

profile of v0, /device:TPU:0, one launch (start us, length us, event | category | flops | bytes accessed | tf_op | source)
XLA Modules:
  0.0 721.8 jit_solution(7972578319023650568)
XLA Ops:
  15.0 123.7 %all-gather.2.cloned.1.call-done = bf16[256,256,128]{2,1,0:T(8,128)(2,1)} async-done(((bf16[16,256,128]{2,1,0:T(8,128)(2,1)}), bf16[256,256,128]{2,1,0:T(8,128)(2,1)}) %all-gather.2.cloned.1.call-update) | async-done | bytes 16777232 | tf_op jit(solution)/shard_map/all_gather | solution.py:25
  138.7 575.3 %while.10 = (s32[]{:T(128)}, bf16[16,256,128]{2,1,0:T(8,128)(2,1)S(1)}, s32[16,64]{1,0:T(8,128)}, bf16[16,256,128]{2,1,0:T(8,128)(2,1)}, s32[16,64]{1,0:T(8,128)S(1)}, /*index=5*/bf16[256,256,128]{2,1,0:T(8,128)(2,1)}, s32[]{:T(128)}) while((s32[]{:T(128)}, bf16[16,256,128]{2,1,0:T(8,128)(2,1)S(1)}, s32[16,64]{1,0:T(8,128)}, ...), condition=%wide.region_3.4_spmd, body=%wide.region_0.3_spmd.sunk | while | flops 2181071616 | bytes 84093936 | solution.py:32
  138.7 8.9 %gather_fusion = bf16[64,256,128]{2,1,0:T(8,128)(2,1)} fusion(bf16[256,256,128]{2,1,0:T(8,128)(2,1)} %get-tuple-element.112, s32[1024]{0:T(1024)S(1)} %pad_clamp_fusion.2), kind=kCustom, calls=%fused_computation.clone.1 | custom fusion | bytes 8388864 | tf_op jit(solution)/shard_map/while/body/eval_jaxpr/gather | solution.py:29
  148.4 10.4 %fusion.23 = (f32[256]{0:T(256)S(1)}, f32[256,16384]{1,0:T(8,128)}) fusion(bf16[16384,128]{1,0:T(8,128)(2,1)} %bitcast.38, bf16[16,256,128]{2,1,0:T(8,128)(2,1)} %get-tuple-element.110, s32[]{:T(128)} %get-tuple-element.100, pred[16384]{0:T(1024)(128)(4,1)S(1)} %broadcast_in_dim.37), kind=kOutput, calls=%fused_computation.23.clone.1 | convolution fusion | flops 1086324480 | bytes 21054976 | tf_op jit(solution)/shard_map/while/body/eval_jaxpr/dot_general | solution.py:10
  158.9 8.1 %fusion.24 = f32[256]{0:T(256)S(1)} fusion(f32[256,16384]{1,0:T(8,128)} %get-tuple-element.91, f32[256]{0:T(256)S(1)} %get-tuple-element.92), kind=kLoop, calls=%fused_computation.6.clone.1 | loop fusion | flops 8388352 | bytes 16779264 | tf_op jit(solution)/shard_map/while/body/eval_jaxpr/reduce_sum | solution.py:17
  167.0 7.6 %fusion.25 = bf16[16,256,128]{2,1,0:T(8,128)(2,1)S(1)} fusion(bf16[16,256,128]{2,1,0:T(8,128)(2,1)S(1)} %get-tuple-element.101, s32[]{:T(128)} %get-tuple-element.100, bf16[16384,128]{1,0:T(8,128)(2,1)S(1)} %bitcast.39, f32[256,16384]{1,0:T(8,128)} %get-tuple-element.91, f32[256]{0:T(256)S(1)} %fusion.24, f32[256]{0:T(256)S(1)} %get-tuple-element.92), kind=kOutput, calls=%fused_computation.10.clone.1 | convolution fusion | flops 1086357504 | bytes 21039108 | tf_op jit(solution)/shard_map/while/body/eval_jaxpr/dot_general | solution.py:19
  174.7 8.9 %gather_fusion = bf16[64,256,128]{2,1,0:T(8,128)(2,1)} fusion(bf16[256,256,128]{2,1,0:T(8,128)(2,1)} %get-tuple-element.112, s32[1024]{0:T(1024)S(1)} %pad_clamp_fusion.2), kind=kCustom, calls=%fused_computation.clone.1 | custom fusion | bytes 8388864 | tf_op jit(solution)/shard_map/while/body/eval_jaxpr/gather | solution.py:29
  184.4 10.4 %fusion.23 = (f32[256]{0:T(256)S(1)}, f32[256,16384]{1,0:T(8,128)}) fusion(bf16[16384,128]{1,0:T(8,128)(2,1)} %bitcast.38, bf16[16,256,128]{2,1,0:T(8,128)(2,1)} %get-tuple-element.110, s32[]{:T(128)} %get-tuple-element.100, pred[16384]{0:T(1024)(128)(4,1)S(1)} %broadcast_in_dim.37), kind=kOutput, calls=%fused_computation.23.clone.1 | convolution fusion | flops 1086324480 | bytes 21054976 | tf_op jit(solution)/shard_map/while/body/eval_jaxpr/dot_general | solution.py:10
  194.8 8.1 %fusion.24 = f32[256]{0:T(256)S(1)} fusion(f32[256,16384]{1,0:T(8,128)} %get-tuple-element.91, f32[256]{0:T(256)S(1)} %get-tuple-element.92), kind=kLoop, calls=%fused_computation.6.clone.1 | loop fusion | flops 8388352 | bytes 16779264 | tf_op jit(solution)/shard_map/while/body/eval_jaxpr/reduce_sum | solution.py:17
  203.0 7.6 %fusion.25 = bf16[16,256,128]{2,1,0:T(8,128)(2,1)S(1)} fusion(bf16[16,256,128]{2,1,0:T(8,128)(2,1)S(1)} %get-tuple-element.101, s32[]{:T(128)} %get-tuple-element.100, bf16[16384,128]{1,0:T(8,128)(2,1)S(1)} %bitcast.39, f32[256,16384]{1,0:T(8,128)} %get-tuple-element.91, f32[256]{0:T(256)S(1)} %fusion.24, f32[256]{0:T(256)S(1)} %get-tuple-element.92), kind=kOutput, calls=%fused_computation.10.clone.1 | convolution fusion | flops 1086357504 | bytes 21039108 | tf_op jit(solution)/shard_map/while/body/eval_jaxpr/dot_general | solution.py:19
  210.6 8.9 %gather_fusion = bf16[64,256,128]{2,1,0:T(8,128)(2,1)} fusion(bf16[256,256,128]{2,1,0:T(8,128)(2,1)} %get-tuple-element.112, s32[1024]{0:T(1024)S(1)} %pad_clamp_fusion.2), kind=kCustom, calls=%fused_computation.clone.1 | custom fusion | bytes 8388864 | tf_op jit(solution)/shard_map/while/body/eval_jaxpr/gather | solution.py:29
  220.3 10.4 %fusion.23 = (f32[256]{0:T(256)S(1)}, f32[256,16384]{1,0:T(8,128)}) fusion(bf16[16384,128]{1,0:T(8,128)(2,1)} %bitcast.38, bf16[16,256,128]{2,1,0:T(8,128)(2,1)} %get-tuple-element.110, s32[]{:T(128)} %get-tuple-element.100, pred[16384]{0:T(1024)(128)(4,1)S(1)} %broadcast_in_dim.37), kind=kOutput, calls=%fused_computation.23.clone.1 | convolution fusion | flops 1086324480 | bytes 21054976 | tf_op jit(solution)/shard_map/while/body/eval_jaxpr/dot_general | solution.py:10
  230.8 8.1 %fusion.24 = f32[256]{0:T(256)S(1)} fusion(f32[256,16384]{1,0:T(8,128)} %get-tuple-element.91, f32[256]{0:T(256)S(1)} %get-tuple-element.92), kind=kLoop, calls=%fused_computation.6.clone.1 | loop fusion | flops 8388352 | bytes 16779264 | tf_op jit(solution)/shard_map/while/body/eval_jaxpr/reduce_sum | solution.py:17
  238.9 7.6 %fusion.25 = bf16[16,256,128]{2,1,0:T(8,128)(2,1)S(1)} fusion(bf16[16,256,128]{2,1,0:T(8,128)(2,1)S(1)} %get-tuple-element.101, s32[]{:T(128)} %get-tuple-element.100, bf16[16384,128]{1,0:T(8,128)(2,1)S(1)} %bitcast.39, f32[256,16384]{1,0:T(8,128)} %get-tuple-element.91, f32[256]{0:T(256)S(1)} %fusion.24, f32[256]{0:T(256)S(1)} %get-tuple-element.92), kind=kOutput, calls=%fused_computation.10.clone.1 | convolution fusion | flops 1086357504 | bytes 21039108 | tf_op jit(solution)/shard_map/while/body/eval_jaxpr/dot_general | solution.py:19
  246.6 8.9 %gather_fusion = bf16[64,256,128]{2,1,0:T(8,128)(2,1)} fusion(bf16[256,256,128]{2,1,0:T(8,128)(2,1)} %get-tuple-element.112, s32[1024]{0:T(1024)S(1)} %pad_clamp_fusion.2), kind=kCustom, calls=%fused_computation.clone.1 | custom fusion | bytes 8388864 | tf_op jit(solution)/shard_map/while/body/eval_jaxpr/gather | solution.py:29
  256.3 10.4 %fusion.23 = (f32[256]{0:T(256)S(1)}, f32[256,16384]{1,0:T(8,128)}) fusion(bf16[16384,128]{1,0:T(8,128)(2,1)} %bitcast.38, bf16[16,256,128]{2,1,0:T(8,128)(2,1)} %get-tuple-element.110, s32[]{:T(128)} %get-tuple-element.100, pred[16384]{0:T(1024)(128)(4,1)S(1)} %broadcast_in_dim.37), kind=kOutput, calls=%fused_computation.23.clone.1 | convolution fusion | flops 1086324480 | bytes 21054976 | tf_op jit(solution)/shard_map/while/body/eval_jaxpr/dot_general | solution.py:10
  266.7 8.1 %fusion.24 = f32[256]{0:T(256)S(1)} fusion(f32[256,16384]{1,0:T(8,128)} %get-tuple-element.91, f32[256]{0:T(256)S(1)} %get-tuple-element.92), kind=kLoop, calls=%fused_computation.6.clone.1 | loop fusion | flops 8388352 | bytes 16779264 | tf_op jit(solution)/shard_map/while/body/eval_jaxpr/reduce_sum | solution.py:17
  274.9 7.6 %fusion.25 = bf16[16,256,128]{2,1,0:T(8,128)(2,1)S(1)} fusion(bf16[16,256,128]{2,1,0:T(8,128)(2,1)S(1)} %get-tuple-element.101, s32[]{:T(128)} %get-tuple-element.100, bf16[16384,128]{1,0:T(8,128)(2,1)S(1)} %bitcast.39, f32[256,16384]{1,0:T(8,128)} %get-tuple-element.91, f32[256]{0:T(256)S(1)} %fusion.24, f32[256]{0:T(256)S(1)} %get-tuple-element.92), kind=kOutput, calls=%fused_computation.10.clone.1 | convolution fusion | flops 1086357504 | bytes 21039108 | tf_op jit(solution)/shard_map/while/body/eval_jaxpr/dot_general | solution.py:19
  282.5 8.9 %gather_fusion = bf16[64,256,128]{2,1,0:T(8,128)(2,1)} fusion(bf16[256,256,128]{2,1,0:T(8,128)(2,1)} %get-tuple-element.112, s32[1024]{0:T(1024)S(1)} %pad_clamp_fusion.2), kind=kCustom, calls=%fused_computation.clone.1 | custom fusion | bytes 8388864 | tf_op jit(solution)/shard_map/while/body/eval_jaxpr/gather | solution.py:29
  292.2 10.4 %fusion.23 = (f32[256]{0:T(256)S(1)}, f32[256,16384]{1,0:T(8,128)}) fusion(bf16[16384,128]{1,0:T(8,128)(2,1)} %bitcast.38, bf16[16,256,128]{2,1,0:T(8,128)(2,1)} %get-tuple-element.110, s32[]{:T(128)} %get-tuple-element.100, pred[16384]{0:T(1024)(128)(4,1)S(1)} %broadcast_in_dim.37), kind=kOutput, calls=%fused_computation.23.clone.1 | convolution fusion | flops 1086324480 | bytes 21054976 | tf_op jit(solution)/shard_map/while/body/eval_jaxpr/dot_general | solution.py:10
  302.7 8.1 %fusion.24 = f32[256]{0:T(256)S(1)} fusion(f32[256,16384]{1,0:T(8,128)} %get-tuple-element.91, f32[256]{0:T(256)S(1)} %get-tuple-element.92), kind=kLoop, calls=%fused_computation.6.clone.1 | loop fusion | flops 8388352 | bytes 16779264 | tf_op jit(solution)/shard_map/while/body/eval_jaxpr/reduce_sum | solution.py:17
  310.8 7.6 %fusion.25 = bf16[16,256,128]{2,1,0:T(8,128)(2,1)S(1)} fusion(bf16[16,256,128]{2,1,0:T(8,128)(2,1)S(1)} %get-tuple-element.101, s32[]{:T(128)} %get-tuple-element.100, bf16[16384,128]{1,0:T(8,128)(2,1)S(1)} %bitcast.39, f32[256,16384]{1,0:T(8,128)} %get-tuple-element.91, f32[256]{0:T(256)S(1)} %fusion.24, f32[256]{0:T(256)S(1)} %get-tuple-element.92), kind=kOutput, calls=%fused_computation.10.clone.1 | convolution fusion | flops 1086357504 | bytes 21039108 | tf_op jit(solution)/shard_map/while/body/eval_jaxpr/dot_general | solution.py:19
  318.5 8.9 %gather_fusion = bf16[64,256,128]{2,1,0:T(8,128)(2,1)} fusion(bf16[256,256,128]{2,1,0:T(8,128)(2,1)} %get-tuple-element.112, s32[1024]{0:T(1024)S(1)} %pad_clamp_fusion.2), kind=kCustom, calls=%fused_computation.clone.1 | custom fusion | bytes 8388864 | tf_op jit(solution)/shard_map/while/body/eval_jaxpr/gather | solution.py:29
  328.2 10.4 %fusion.23 = (f32[256]{0:T(256)S(1)}, f32[256,16384]{1,0:T(8,128)}) fusion(bf16[16384,128]{1,0:T(8,128)(2,1)} %bitcast.38, bf16[16,256,128]{2,1,0:T(8,128)(2,1)} %get-tuple-element.110, s32[]{:T(128)} %get-tuple-element.100, pred[16384]{0:T(1024)(128)(4,1)S(1)} %broadcast_in_dim.37), kind=kOutput, calls=%fused_computation.23.clone.1 | convolution fusion | flops 1086324480 | bytes 21054976 | tf_op jit(solution)/shard_map/while/body/eval_jaxpr/dot_general | solution.py:10
  338.6 8.1 %fusion.24 = f32[256]{0:T(256)S(1)} fusion(f32[256,16384]{1,0:T(8,128)} %get-tuple-element.91, f32[256]{0:T(256)S(1)} %get-tuple-element.92), kind=kLoop, calls=%fused_computation.6.clone.1 | loop fusion | flops 8388352 | bytes 16779264 | tf_op jit(solution)/shard_map/while/body/eval_jaxpr/reduce_sum | solution.py:17
  346.8 7.6 %fusion.25 = bf16[16,256,128]{2,1,0:T(8,128)(2,1)S(1)} fusion(bf16[16,256,128]{2,1,0:T(8,128)(2,1)S(1)} %get-tuple-element.101, s32[]{:T(128)} %get-tuple-element.100, bf16[16384,128]{1,0:T(8,128)(2,1)S(1)} %bitcast.39, f32[256,16384]{1,0:T(8,128)} %get-tuple-element.91, f32[256]{0:T(256)S(1)} %fusion.24, f32[256]{0:T(256)S(1)} %get-tuple-element.92), kind=kOutput, calls=%fused_computation.10.clone.1 | convolution fusion | flops 1086357504 | bytes 21039108 | tf_op jit(solution)/shard_map/while/body/eval_jaxpr/dot_general | solution.py:19
  354.5 8.9 %gather_fusion = bf16[64,256,128]{2,1,0:T(8,128)(2,1)} fusion(bf16[256,256,128]{2,1,0:T(8,128)(2,1)} %get-tuple-element.112, s32[1024]{0:T(1024)S(1)} %pad_clamp_fusion.2), kind=kCustom, calls=%fused_computation.clone.1 | custom fusion | bytes 8388864 | tf_op jit(solution)/shard_map/while/body/eval_jaxpr/gather | solution.py:29
  364.2 10.4 %fusion.23 = (f32[256]{0:T(256)S(1)}, f32[256,16384]{1,0:T(8,128)}) fusion(bf16[16384,128]{1,0:T(8,128)(2,1)} %bitcast.38, bf16[16,256,128]{2,1,0:T(8,128)(2,1)} %get-tuple-element.110, s32[]{:T(128)} %get-tuple-element.100, pred[16384]{0:T(1024)(128)(4,1)S(1)} %broadcast_in_dim.37), kind=kOutput, calls=%fused_computation.23.clone.1 | convolution fusion | flops 1086324480 | bytes 21054976 | tf_op jit(solution)/shard_map/while/body/eval_jaxpr/dot_general | solution.py:10
  374.6 8.1 %fusion.24 = f32[256]{0:T(256)S(1)} fusion(f32[256,16384]{1,0:T(8,128)} %get-tuple-element.91, f32[256]{0:T(256)S(1)} %get-tuple-element.92), kind=kLoop, calls=%fused_computation.6.clone.1 | loop fusion | flops 8388352 | bytes 16779264 | tf_op jit(solution)/shard_map/while/body/eval_jaxpr/reduce_sum | solution.py:17
  382.8 7.6 %fusion.25 = bf16[16,256,128]{2,1,0:T(8,128)(2,1)S(1)} fusion(bf16[16,256,128]{2,1,0:T(8,128)(2,1)S(1)} %get-tuple-element.101, s32[]{:T(128)} %get-tuple-element.100, bf16[16384,128]{1,0:T(8,128)(2,1)S(1)} %bitcast.39, f32[256,16384]{1,0:T(8,128)} %get-tuple-element.91, f32[256]{0:T(256)S(1)} %fusion.24, f32[256]{0:T(256)S(1)} %get-tuple-element.92), kind=kOutput, calls=%fused_computation.10.clone.1 | convolution fusion | flops 1086357504 | bytes 21039108 | tf_op jit(solution)/shard_map/while/body/eval_jaxpr/dot_general | solution.py:19
  390.4 8.9 %gather_fusion = bf16[64,256,128]{2,1,0:T(8,128)(2,1)} fusion(bf16[256,256,128]{2,1,0:T(8,128)(2,1)} %get-tuple-element.112, s32[1024]{0:T(1024)S(1)} %pad_clamp_fusion.2), kind=kCustom, calls=%fused_computation.clone.1 | custom fusion | bytes 8388864 | tf_op jit(solution)/shard_map/while/body/eval_jaxpr/gather | solution.py:29
  400.1 10.4 %fusion.23 = (f32[256]{0:T(256)S(1)}, f32[256,16384]{1,0:T(8,128)}) fusion(bf16[16384,128]{1,0:T(8,128)(2,1)} %bitcast.38, bf16[16,256,128]{2,1,0:T(8,128)(2,1)} %get-tuple-element.110, s32[]{:T(128)} %get-tuple-element.100, pred[16384]{0:T(1024)(128)(4,1)S(1)} %broadcast_in_dim.37), kind=kOutput, calls=%fused_computation.23.clone.1 | convolution fusion | flops 1086324480 | bytes 21054976 | tf_op jit(solution)/shard_map/while/body/eval_jaxpr/dot_general | solution.py:10
  410.6 8.1 %fusion.24 = f32[256]{0:T(256)S(1)} fusion(f32[256,16384]{1,0:T(8,128)} %get-tuple-element.91, f32[256]{0:T(256)S(1)} %get-tuple-element.92), kind=kLoop, calls=%fused_computation.6.clone.1 | loop fusion | flops 8388352 | bytes 16779264 | tf_op jit(solution)/shard_map/while/body/eval_jaxpr/reduce_sum | solution.py:17
  418.7 7.6 %fusion.25 = bf16[16,256,128]{2,1,0:T(8,128)(2,1)S(1)} fusion(bf16[16,256,128]{2,1,0:T(8,128)(2,1)S(1)} %get-tuple-element.101, s32[]{:T(128)} %get-tuple-element.100, bf16[16384,128]{1,0:T(8,128)(2,1)S(1)} %bitcast.39, f32[256,16384]{1,0:T(8,128)} %get-tuple-element.91, f32[256]{0:T(256)S(1)} %fusion.24, f32[256]{0:T(256)S(1)} %get-tuple-element.92), kind=kOutput, calls=%fused_computation.10.clone.1 | convolution fusion | flops 1086357504 | bytes 21039108 | tf_op jit(solution)/shard_map/while/body/eval_jaxpr/dot_general | solution.py:19
  426.4 8.9 %gather_fusion = bf16[64,256,128]{2,1,0:T(8,128)(2,1)} fusion(bf16[256,256,128]{2,1,0:T(8,128)(2,1)} %get-tuple-element.112, s32[1024]{0:T(1024)S(1)} %pad_clamp_fusion.2), kind=kCustom, calls=%fused_computation.clone.1 | custom fusion | bytes 8388864 | tf_op jit(solution)/shard_map/while/body/eval_jaxpr/gather | solution.py:29
  436.1 10.4 %fusion.23 = (f32[256]{0:T(256)S(1)}, f32[256,16384]{1,0:T(8,128)}) fusion(bf16[16384,128]{1,0:T(8,128)(2,1)} %bitcast.38, bf16[16,256,128]{2,1,0:T(8,128)(2,1)} %get-tuple-element.110, s32[]{:T(128)} %get-tuple-element.100, pred[16384]{0:T(1024)(128)(4,1)S(1)} %broadcast_in_dim.37), kind=kOutput, calls=%fused_computation.23.clone.1 | convolution fusion | flops 1086324480 | bytes 21054976 | tf_op jit(solution)/shard_map/while/body/eval_jaxpr/dot_general | solution.py:10
  446.5 8.1 %fusion.24 = f32[256]{0:T(256)S(1)} fusion(f32[256,16384]{1,0:T(8,128)} %get-tuple-element.91, f32[256]{0:T(256)S(1)} %get-tuple-element.92), kind=kLoop, calls=%fused_computation.6.clone.1 | loop fusion | flops 8388352 | bytes 16779264 | tf_op jit(solution)/shard_map/while/body/eval_jaxpr/reduce_sum | solution.py:17
  454.7 7.6 %fusion.25 = bf16[16,256,128]{2,1,0:T(8,128)(2,1)S(1)} fusion(bf16[16,256,128]{2,1,0:T(8,128)(2,1)S(1)} %get-tuple-element.101, s32[]{:T(128)} %get-tuple-element.100, bf16[16384,128]{1,0:T(8,128)(2,1)S(1)} %bitcast.39, f32[256,16384]{1,0:T(8,128)} %get-tuple-element.91, f32[256]{0:T(256)S(1)} %fusion.24, f32[256]{0:T(256)S(1)} %get-tuple-element.92), kind=kOutput, calls=%fused_computation.10.clone.1 | convolution fusion | flops 1086357504 | bytes 21039108 | tf_op jit(solution)/shard_map/while/body/eval_jaxpr/dot_general | solution.py:19
  462.3 8.9 %gather_fusion = bf16[64,256,128]{2,1,0:T(8,128)(2,1)} fusion(bf16[256,256,128]{2,1,0:T(8,128)(2,1)} %get-tuple-element.112, s32[1024]{0:T(1024)S(1)} %pad_clamp_fusion.2), kind=kCustom, calls=%fused_computation.clone.1 | custom fusion | bytes 8388864 | tf_op jit(solution)/shard_map/while/body/eval_jaxpr/gather | solution.py:29
  472.0 10.4 %fusion.23 = (f32[256]{0:T(256)S(1)}, f32[256,16384]{1,0:T(8,128)}) fusion(bf16[16384,128]{1,0:T(8,128)(2,1)} %bitcast.38, bf16[16,256,128]{2,1,0:T(8,128)(2,1)} %get-tuple-element.110, s32[]{:T(128)} %get-tuple-element.100, pred[16384]{0:T(1024)(128)(4,1)S(1)} %broadcast_in_dim.37), kind=kOutput, calls=%fused_computation.23.clone.1 | convolution fusion | flops 1086324480 | bytes 21054976 | tf_op jit(solution)/shard_map/while/body/eval_jaxpr/dot_general | solution.py:10
  482.5 8.1 %fusion.24 = f32[256]{0:T(256)S(1)} fusion(f32[256,16384]{1,0:T(8,128)} %get-tuple-element.91, f32[256]{0:T(256)S(1)} %get-tuple-element.92), kind=kLoop, calls=%fused_computation.6.clone.1 | loop fusion | flops 8388352 | bytes 16779264 | tf_op jit(solution)/shard_map/while/body/eval_jaxpr/reduce_sum | solution.py:17
  490.6 7.6 %fusion.25 = bf16[16,256,128]{2,1,0:T(8,128)(2,1)S(1)} fusion(bf16[16,256,128]{2,1,0:T(8,128)(2,1)S(1)} %get-tuple-element.101, s32[]{:T(128)} %get-tuple-element.100, bf16[16384,128]{1,0:T(8,128)(2,1)S(1)} %bitcast.39, f32[256,16384]{1,0:T(8,128)} %get-tuple-element.91, f32[256]{0:T(256)S(1)} %fusion.24, f32[256]{0:T(256)S(1)} %get-tuple-element.92), kind=kOutput, calls=%fused_computation.10.clone.1 | convolution fusion | flops 1086357504 | bytes 21039108 | tf_op jit(solution)/shard_map/while/body/eval_jaxpr/dot_general | solution.py:19
  498.3 8.9 %gather_fusion = bf16[64,256,128]{2,1,0:T(8,128)(2,1)} fusion(bf16[256,256,128]{2,1,0:T(8,128)(2,1)} %get-tuple-element.112, s32[1024]{0:T(1024)S(1)} %pad_clamp_fusion.2), kind=kCustom, calls=%fused_computation.clone.1 | custom fusion | bytes 8388864 | tf_op jit(solution)/shard_map/while/body/eval_jaxpr/gather | solution.py:29
  508.0 10.4 %fusion.23 = (f32[256]{0:T(256)S(1)}, f32[256,16384]{1,0:T(8,128)}) fusion(bf16[16384,128]{1,0:T(8,128)(2,1)} %bitcast.38, bf16[16,256,128]{2,1,0:T(8,128)(2,1)} %get-tuple-element.110, s32[]{:T(128)} %get-tuple-element.100, pred[16384]{0:T(1024)(128)(4,1)S(1)} %broadcast_in_dim.37), kind=kOutput, calls=%fused_computation.23.clone.1 | convolution fusion | flops 1086324480 | bytes 21054976 | tf_op jit(solution)/shard_map/while/body/eval_jaxpr/dot_general | solution.py:10
  518.4 8.1 %fusion.24 = f32[256]{0:T(256)S(1)} fusion(f32[256,16384]{1,0:T(8,128)} %get-tuple-element.91, f32[256]{0:T(256)S(1)} %get-tuple-element.92), kind=kLoop, calls=%fused_computation.6.clone.1 | loop fusion | flops 8388352 | bytes 16779264 | tf_op jit(solution)/shard_map/while/body/eval_jaxpr/reduce_sum | solution.py:17
  526.6 7.6 %fusion.25 = bf16[16,256,128]{2,1,0:T(8,128)(2,1)S(1)} fusion(bf16[16,256,128]{2,1,0:T(8,128)(2,1)S(1)} %get-tuple-element.101, s32[]{:T(128)} %get-tuple-element.100, bf16[16384,128]{1,0:T(8,128)(2,1)S(1)} %bitcast.39, f32[256,16384]{1,0:T(8,128)} %get-tuple-element.91, f32[256]{0:T(256)S(1)} %fusion.24, f32[256]{0:T(256)S(1)} %get-tuple-element.92), kind=kOutput, calls=%fused_computation.10.clone.1 | convolution fusion | flops 1086357504 | bytes 21039108 | tf_op jit(solution)/shard_map/while/body/eval_jaxpr/dot_general | solution.py:19
  534.2 8.9 %gather_fusion = bf16[64,256,128]{2,1,0:T(8,128)(2,1)} fusion(bf16[256,256,128]{2,1,0:T(8,128)(2,1)} %get-tuple-element.112, s32[1024]{0:T(1024)S(1)} %pad_clamp_fusion.2), kind=kCustom, calls=%fused_computation.clone.1 | custom fusion | bytes 8388864 | tf_op jit(solution)/shard_map/while/body/eval_jaxpr/gather | solution.py:29
  544.0 10.4 %fusion.23 = (f32[256]{0:T(256)S(1)}, f32[256,16384]{1,0:T(8,128)}) fusion(bf16[16384,128]{1,0:T(8,128)(2,1)} %bitcast.38, bf16[16,256,128]{2,1,0:T(8,128)(2,1)} %get-tuple-element.110, s32[]{:T(128)} %get-tuple-element.100, pred[16384]{0:T(1024)(128)(4,1)S(1)} %broadcast_in_dim.37), kind=kOutput, calls=%fused_computation.23.clone.1 | convolution fusion | flops 1086324480 | bytes 21054976 | tf_op jit(solution)/shard_map/while/body/eval_jaxpr/dot_general | solution.py:10
  554.4 8.1 %fusion.24 = f32[256]{0:T(256)S(1)} fusion(f32[256,16384]{1,0:T(8,128)} %get-tuple-element.91, f32[256]{0:T(256)S(1)} %get-tuple-element.92), kind=kLoop, calls=%fused_computation.6.clone.1 | loop fusion | flops 8388352 | bytes 16779264 | tf_op jit(solution)/shard_map/while/body/eval_jaxpr/reduce_sum | solution.py:17
  562.5 7.6 %fusion.25 = bf16[16,256,128]{2,1,0:T(8,128)(2,1)S(1)} fusion(bf16[16,256,128]{2,1,0:T(8,128)(2,1)S(1)} %get-tuple-element.101, s32[]{:T(128)} %get-tuple-element.100, bf16[16384,128]{1,0:T(8,128)(2,1)S(1)} %bitcast.39, f32[256,16384]{1,0:T(8,128)} %get-tuple-element.91, f32[256]{0:T(256)S(1)} %fusion.24, f32[256]{0:T(256)S(1)} %get-tuple-element.92), kind=kOutput, calls=%fused_computation.10.clone.1 | convolution fusion | flops 1086357504 | bytes 21039108 | tf_op jit(solution)/shard_map/while/body/eval_jaxpr/dot_general | solution.py:19
  570.2 8.9 %gather_fusion = bf16[64,256,128]{2,1,0:T(8,128)(2,1)} fusion(bf16[256,256,128]{2,1,0:T(8,128)(2,1)} %get-tuple-element.112, s32[1024]{0:T(1024)S(1)} %pad_clamp_fusion.2), kind=kCustom, calls=%fused_computation.clone.1 | custom fusion | bytes 8388864 | tf_op jit(solution)/shard_map/while/body/eval_jaxpr/gather | solution.py:29
  579.9 10.4 %fusion.23 = (f32[256]{0:T(256)S(1)}, f32[256,16384]{1,0:T(8,128)}) fusion(bf16[16384,128]{1,0:T(8,128)(2,1)} %bitcast.38, bf16[16,256,128]{2,1,0:T(8,128)(2,1)} %get-tuple-element.110, s32[]{:T(128)} %get-tuple-element.100, pred[16384]{0:T(1024)(128)(4,1)S(1)} %broadcast_in_dim.37), kind=kOutput, calls=%fused_computation.23.clone.1 | convolution fusion | flops 1086324480 | bytes 21054976 | tf_op jit(solution)/shard_map/while/body/eval_jaxpr/dot_general | solution.py:10
  590.4 8.1 %fusion.24 = f32[256]{0:T(256)S(1)} fusion(f32[256,16384]{1,0:T(8,128)} %get-tuple-element.91, f32[256]{0:T(256)S(1)} %get-tuple-element.92), kind=kLoop, calls=%fused_computation.6.clone.1 | loop fusion | flops 8388352 | bytes 16779264 | tf_op jit(solution)/shard_map/while/body/eval_jaxpr/reduce_sum | solution.py:17
  598.5 7.6 %fusion.25 = bf16[16,256,128]{2,1,0:T(8,128)(2,1)S(1)} fusion(bf16[16,256,128]{2,1,0:T(8,128)(2,1)S(1)} %get-tuple-element.101, s32[]{:T(128)} %get-tuple-element.100, bf16[16384,128]{1,0:T(8,128)(2,1)S(1)} %bitcast.39, f32[256,16384]{1,0:T(8,128)} %get-tuple-element.91, f32[256]{0:T(256)S(1)} %fusion.24, f32[256]{0:T(256)S(1)} %get-tuple-element.92), kind=kOutput, calls=%fused_computation.10.clone.1 | convolution fusion | flops 1086357504 | bytes 21039108 | tf_op jit(solution)/shard_map/while/body/eval_jaxpr/dot_general | solution.py:19
  606.2 8.9 %gather_fusion = bf16[64,256,128]{2,1,0:T(8,128)(2,1)} fusion(bf16[256,256,128]{2,1,0:T(8,128)(2,1)} %get-tuple-element.112, s32[1024]{0:T(1024)S(1)} %pad_clamp_fusion.2), kind=kCustom, calls=%fused_computation.clone.1 | custom fusion | bytes 8388864 | tf_op jit(solution)/shard_map/while/body/eval_jaxpr/gather | solution.py:29
  615.9 10.4 %fusion.23 = (f32[256]{0:T(256)S(1)}, f32[256,16384]{1,0:T(8,128)}) fusion(bf16[16384,128]{1,0:T(8,128)(2,1)} %bitcast.38, bf16[16,256,128]{2,1,0:T(8,128)(2,1)} %get-tuple-element.110, s32[]{:T(128)} %get-tuple-element.100, pred[16384]{0:T(1024)(128)(4,1)S(1)} %broadcast_in_dim.37), kind=kOutput, calls=%fused_computation.23.clone.1 | convolution fusion | flops 1086324480 | bytes 21054976 | tf_op jit(solution)/shard_map/while/body/eval_jaxpr/dot_general | solution.py:10
  626.3 8.1 %fusion.24 = f32[256]{0:T(256)S(1)} fusion(f32[256,16384]{1,0:T(8,128)} %get-tuple-element.91, f32[256]{0:T(256)S(1)} %get-tuple-element.92), kind=kLoop, calls=%fused_computation.6.clone.1 | loop fusion | flops 8388352 | bytes 16779264 | tf_op jit(solution)/shard_map/while/body/eval_jaxpr/reduce_sum | solution.py:17
  642.1 8.9 %gather_fusion = bf16[64,256,128]{2,1,0:T(8,128)(2,1)} fusion(bf16[256,256,128]{2,1,0:T(8,128)(2,1)} %get-tuple-element.112, s32[1024]{0:T(1024)S(1)} %pad_clamp_fusion.2), kind=kCustom, calls=%fused_computation.clone.1 | custom fusion | bytes 8388864 | tf_op jit(solution)/shard_map/while/body/eval_jaxpr/gather | solution.py:29
  651.8 10.4 %fusion.23 = (f32[256]{0:T(256)S(1)}, f32[256,16384]{1,0:T(8,128)}) fusion(bf16[16384,128]{1,0:T(8,128)(2,1)} %bitcast.38, bf16[16,256,128]{2,1,0:T(8,128)(2,1)} %get-tuple-element.110, s32[]{:T(128)} %get-tuple-element.100, pred[16384]{0:T(1024)(128)(4,1)S(1)} %broadcast_in_dim.37), kind=kOutput, calls=%fused_computation.23.clone.1 | convolution fusion | flops 1086324480 | bytes 21054976 | tf_op jit(solution)/shard_map/while/body/eval_jaxpr/dot_general | solution.py:10
  662.3 8.1 %fusion.24 = f32[256]{0:T(256)S(1)} fusion(f32[256,16384]{1,0:T(8,128)} %get-tuple-element.91, f32[256]{0:T(256)S(1)} %get-tuple-element.92), kind=kLoop, calls=%fused_computation.6.clone.1 | loop fusion | flops 8388352 | bytes 16779264 | tf_op jit(solution)/shard_map/while/body/eval_jaxpr/reduce_sum | solution.py:17
  678.1 8.9 %gather_fusion = bf16[64,256,128]{2,1,0:T(8,128)(2,1)} fusion(bf16[256,256,128]{2,1,0:T(8,128)(2,1)} %get-tuple-element.112, s32[1024]{0:T(1024)S(1)} %pad_clamp_fusion.2), kind=kCustom, calls=%fused_computation.clone.1 | custom fusion | bytes 8388864 | tf_op jit(solution)/shard_map/while/body/eval_jaxpr/gather | solution.py:29
  687.8 10.4 %fusion.23 = (f32[256]{0:T(256)S(1)}, f32[256,16384]{1,0:T(8,128)}) fusion(bf16[16384,128]{1,0:T(8,128)(2,1)} %bitcast.38, bf16[16,256,128]{2,1,0:T(8,128)(2,1)} %get-tuple-element.110, s32[]{:T(128)} %get-tuple-element.100, pred[16384]{0:T(1024)(128)(4,1)S(1)} %broadcast_in_dim.37), kind=kOutput, calls=%fused_computation.23.clone.1 | convolution fusion | flops 1086324480 | bytes 21054976 | tf_op jit(solution)/shard_map/while/body/eval_jaxpr/dot_general | solution.py:10
  698.2 8.1 %fusion.24 = f32[256]{0:T(256)S(1)} fusion(f32[256,16384]{1,0:T(8,128)} %get-tuple-element.91, f32[256]{0:T(256)S(1)} %get-tuple-element.92), kind=kLoop, calls=%fused_computation.6.clone.1 | loop fusion | flops 8388352 | bytes 16779264 | tf_op jit(solution)/shard_map/while/body/eval_jaxpr/reduce_sum | solution.py:17
  706.4 7.6 %fusion.25 = bf16[16,256,128]{2,1,0:T(8,128)(2,1)S(1)} fusion(bf16[16,256,128]{2,1,0:T(8,128)(2,1)S(1)} %get-tuple-element.101, s32[]{:T(128)} %get-tuple-element.100, bf16[16384,128]{1,0:T(8,128)(2,1)S(1)} %bitcast.39, f32[256,16384]{1,0:T(8,128)} %get-tuple-element.91, f32[256]{0:T(256)S(1)} %fusion.24, f32[256]{0:T(256)S(1)} %get-tuple-element.92), kind=kOutput, calls=%fused_computation.10.clone.1 | convolution fusion | flops 1086357504 | bytes 21039108 | tf_op jit(solution)/shard_map/while/body/eval_jaxpr/dot_general | solution.py:19
  (126 shorter events, 37.6 us)
Async XLA Ops:
  6.5 1.5 copy-start
  6.5 132.1 %all-gather.2.cloned.1.call-start = ((), (), s32[]{:S(2)}) async-start(), calls=%async_computation | async-start | bytes 17825792 | tf_op jit(solution)/shard_map/all_gather | solution.py:25
  148.4 18.6 %copy-start.1 = (bf16[64,256,128]{2,1,0:T(8,128)(2,1)S(1)}, bf16[64,256,128]{2,1,0:T(8,128)(2,1)}, u32[]{:S(2)}) copy-start(bf16[64,256,128]{2,1,0:T(8,128)(2,1)} %gather_fusion) | copy-start | bytes 12582916 | tf_op jit(solution)/shard_map/while
  184.4 18.6 %copy-start.1 = (bf16[64,256,128]{2,1,0:T(8,128)(2,1)S(1)}, bf16[64,256,128]{2,1,0:T(8,128)(2,1)}, u32[]{:S(2)}) copy-start(bf16[64,256,128]{2,1,0:T(8,128)(2,1)} %gather_fusion) | copy-start | bytes 12582916 | tf_op jit(solution)/shard_map/while
  220.3 18.6 %copy-start.1 = (bf16[64,256,128]{2,1,0:T(8,128)(2,1)S(1)}, bf16[64,256,128]{2,1,0:T(8,128)(2,1)}, u32[]{:S(2)}) copy-start(bf16[64,256,128]{2,1,0:T(8,128)(2,1)} %gather_fusion) | copy-start | bytes 12582916 | tf_op jit(solution)/shard_map/while
  256.3 18.6 %copy-start.1 = (bf16[64,256,128]{2,1,0:T(8,128)(2,1)S(1)}, bf16[64,256,128]{2,1,0:T(8,128)(2,1)}, u32[]{:S(2)}) copy-start(bf16[64,256,128]{2,1,0:T(8,128)(2,1)} %gather_fusion) | copy-start | bytes 12582916 | tf_op jit(solution)/shard_map/while
  292.2 18.6 %copy-start.1 = (bf16[64,256,128]{2,1,0:T(8,128)(2,1)S(1)}, bf16[64,256,128]{2,1,0:T(8,128)(2,1)}, u32[]{:S(2)}) copy-start(bf16[64,256,128]{2,1,0:T(8,128)(2,1)} %gather_fusion) | copy-start | bytes 12582916 | tf_op jit(solution)/shard_map/while
  328.2 18.6 %copy-start.1 = (bf16[64,256,128]{2,1,0:T(8,128)(2,1)S(1)}, bf16[64,256,128]{2,1,0:T(8,128)(2,1)}, u32[]{:S(2)}) copy-start(bf16[64,256,128]{2,1,0:T(8,128)(2,1)} %gather_fusion) | copy-start | bytes 12582916 | tf_op jit(solution)/shard_map/while
  364.2 18.6 %copy-start.1 = (bf16[64,256,128]{2,1,0:T(8,128)(2,1)S(1)}, bf16[64,256,128]{2,1,0:T(8,128)(2,1)}, u32[]{:S(2)}) copy-start(bf16[64,256,128]{2,1,0:T(8,128)(2,1)} %gather_fusion) | copy-start | bytes 12582916 | tf_op jit(solution)/shard_map/while
  400.1 18.6 %copy-start.1 = (bf16[64,256,128]{2,1,0:T(8,128)(2,1)S(1)}, bf16[64,256,128]{2,1,0:T(8,128)(2,1)}, u32[]{:S(2)}) copy-start(bf16[64,256,128]{2,1,0:T(8,128)(2,1)} %gather_fusion) | copy-start | bytes 12582916 | tf_op jit(solution)/shard_map/while
  436.1 18.6 %copy-start.1 = (bf16[64,256,128]{2,1,0:T(8,128)(2,1)S(1)}, bf16[64,256,128]{2,1,0:T(8,128)(2,1)}, u32[]{:S(2)}) copy-start(bf16[64,256,128]{2,1,0:T(8,128)(2,1)} %gather_fusion) | copy-start | bytes 12582916 | tf_op jit(solution)/shard_map/while
  472.0 18.6 %copy-start.1 = (bf16[64,256,128]{2,1,0:T(8,128)(2,1)S(1)}, bf16[64,256,128]{2,1,0:T(8,128)(2,1)}, u32[]{:S(2)}) copy-start(bf16[64,256,128]{2,1,0:T(8,128)(2,1)} %gather_fusion) | copy-start | bytes 12582916 | tf_op jit(solution)/shard_map/while
  508.0 18.6 %copy-start.1 = (bf16[64,256,128]{2,1,0:T(8,128)(2,1)S(1)}, bf16[64,256,128]{2,1,0:T(8,128)(2,1)}, u32[]{:S(2)}) copy-start(bf16[64,256,128]{2,1,0:T(8,128)(2,1)} %gather_fusion) | copy-start | bytes 12582916 | tf_op jit(solution)/shard_map/while
  543.9 18.6 %copy-start.1 = (bf16[64,256,128]{2,1,0:T(8,128)(2,1)S(1)}, bf16[64,256,128]{2,1,0:T(8,128)(2,1)}, u32[]{:S(2)}) copy-start(bf16[64,256,128]{2,1,0:T(8,128)(2,1)} %gather_fusion) | copy-start | bytes 12582916 | tf_op jit(solution)/shard_map/while
  579.9 18.6 %copy-start.1 = (bf16[64,256,128]{2,1,0:T(8,128)(2,1)S(1)}, bf16[64,256,128]{2,1,0:T(8,128)(2,1)}, u32[]{:S(2)}) copy-start(bf16[64,256,128]{2,1,0:T(8,128)(2,1)} %gather_fusion) | copy-start | bytes 12582916 | tf_op jit(solution)/shard_map/while
  615.9 18.6 %copy-start.1 = (bf16[64,256,128]{2,1,0:T(8,128)(2,1)S(1)}, bf16[64,256,128]{2,1,0:T(8,128)(2,1)}, u32[]{:S(2)}) copy-start(bf16[64,256,128]{2,1,0:T(8,128)(2,1)} %gather_fusion) | copy-start | bytes 12582916 | tf_op jit(solution)/shard_map/while
  651.8 18.6 %copy-start.1 = (bf16[64,256,128]{2,1,0:T(8,128)(2,1)S(1)}, bf16[64,256,128]{2,1,0:T(8,128)(2,1)}, u32[]{:S(2)}) copy-start(bf16[64,256,128]{2,1,0:T(8,128)(2,1)} %gather_fusion) | copy-start | bytes 12582916 | tf_op jit(solution)/shard_map/while
  687.8 18.6 %copy-start.1 = (bf16[64,256,128]{2,1,0:T(8,128)(2,1)S(1)}, bf16[64,256,128]{2,1,0:T(8,128)(2,1)}, u32[]{:S(2)}) copy-start(bf16[64,256,128]{2,1,0:T(8,128)(2,1)} %gather_fusion) | copy-start | bytes 12582916 | tf_op jit(solution)/shard_map/while
  714.0 1.0 copy-start.2
Sparse Core Ops, SparseCore 0:
  9.5 129.1 all-gather.1
where the time goes:
time: 724 us; the launch traced here: 722 us
  matrix products  289 us (40%)
  local copies, waits for them, and re-layouts  152 us (21%)
  other arithmetic  142 us (20%)
  waiting for transfers between devices  124 us (17%)
  between operations  13.4 us (2%)
    dot_general x16, matrix products, attend_tile(): jnp.dot(tile_query, tile_keys.T, preferred_element_type=jnp.float32)  167 us
    gather x16, local copies, waits for them, and re-layouts, one_tile(): stored = source[chosen].reshape(-1, channels)  142 us
    reduce_sum x16, other arithmetic, attend_tile(): totals = jnp.sum(raised, axis=1, keepdims=True)  130 us
    all_gather x1, waiting for transfers between devices, body(): source = lax.all_gather(target, 'band', axis=0, tiled=True)  124 us
    dot_general x16, matrix products, attend_tile(): jnp.dot(weights, tile_keys, preferred_element_type=jnp.float32)  122 us
  transfers between devices with their start and end apart: 1, of which 1 were waited for; matrix products, arithmetic and copies ran while one was open for 1% of the time, Pallas kernels for 0%

commit v1 on v0

--- a/solution.py
+++ b/solution.py
@@ -3,6 +3,12 @@
 import jax.numpy as jnp
 from jax import lax
 from jax.sharding import PartitionSpec as P
+
+
+def joined_along(parts, dim):
+    shape = list(parts.shape[1:])
+    shape[dim] *= parts.shape[0]
+    return jnp.moveaxis(parts, 0, dim).reshape(shape)
 
 
 def attend_tile(tile_query, tile_keys, keep_mask):
@@ -22,7 +28,19 @@
 def body(query_tiles, target, tile_home, candidates, valid_mask):
     channels = target.shape[2]
     stored_rows = tile_home[candidates]
-    source = lax.all_gather(target, "band", axis=0, tiled=True)
+    size = lax.axis_size("band")
+    pairs = [(i, (i + 1) % size) for i in range(size)]
+    back = [(b, a) for a, b in pairs]
+    lower, upper = ([], [])
+    for hop in range(size - 1):
+        if hop % 2 == 0:
+            lower.append(lax.ppermute(lower[-1] if lower else target, "band", pairs))
+        else:
+            upper.append(lax.ppermute(upper[-1] if upper else target, "band", back))
+    blocks = jnp.stack([*lower[::-1], target, *upper])
+    shift = lax.axis_index("band") - len(lower)
+    blocks = blocks[(jnp.arange(size) - shift) % size]
+    source = joined_along(blocks, 0)
 
     def one_tile(packed):
         tile_query, chosen, keep_mask = packed

time: 724 us -> 810 us (1.12)
  the two profiles are of different devices: /device:TPU:0 before, /device:TPU:1 now
where the time goes in v1:
time: 810 us; the launch traced here: 808 us
  matrix products  289 us (36%)
  local copies, waits for them, and re-layouts  198 us (24%)
  waiting for transfers between devices  157 us (19%)
  other arithmetic  142 us (18%)
  starting transfers between devices  21.2 us (3%)
    dot_general x16, matrix products, attend_tile(): jnp.dot(tile_query, tile_keys.T, preferred_element_type=jnp.float32)  167 us
    gather x16, local copies, waits for them, and re-layouts, one_tile(): stored = source[chosen].reshape(-1, channels)  143 us
    reduce_sum x16, other arithmetic, attend_tile(): totals = jnp.sum(raised, axis=1, keepdims=True)  130 us
    dot_general x16, matrix products, attend_tile(): jnp.dot(weights, tile_keys, preferred_element_type=jnp.float32)  122 us
    ppermute x8, waiting for transfers between devices, body(): lower.append(lax.ppermute(lower[-1] if lower else target, 'band', pairs))  97.7 us
    ppermute x7, waiting for transfers between devices, body(): upper.append(lax.ppermute(upper[-1] if upper else target, 'band', back))  59.5 us
    unnamed x47, local copies, waits for them, and re-layouts  32.1 us
    ppermute x8, starting transfers between devices, body(): lower.append(lax.ppermute(lower[-1] if lower else target, 'band', pairs))  20 us
  transfers between devices with their start and end apart: 15, of which 14 were waited for; matrix products, arithmetic and copies ran while one was open for 4% of the time, Pallas kernels for 0%

profile of v1, /device:TPU:1, one launch (start us, length us, event | category | flops | bytes accessed | tf_op | source)
XLA Modules:
  0.0 808.3 jit_solution(2296152881098622929)
XLA Ops:
  2.6 12.1 %collective-permute-done = bf16[16,256,128]{2,1,0:T(8,128)(2,1)S(1)} collective-permute-done((bf16[16,256,128]{2,1,0:T(8,128)(2,1)}, bf16[16,256,128]{2,1,0:T(8,128)(2,1)S(1)}, u32[]{:S(2)}, u32[]{:S(2)}) %collective-permute-start) | collective-permute-done | bytes 1048608 | tf_op jit(solution)/shard_map/ppermute | solution.py:37
  18.2 21.8 %collective-permute-done.1 = bf16[16,256,128]{2,1,0:T(8,128)(2,1)S(1)} collective-permute-done((bf16[16,256,128]{2,1,0:T(8,128)(2,1)S(1)}, bf16[16,256,128]{2,1,0:T(8,128)(2,1)S(1)}, u32[]{:S(2)}, u32[]{:S(2)}) %collective-permute-start.1) | collective-permute-done | bytes 1048608 | tf_op jit(solution)/shard_map/ppermute | solution.py:37
  42.5 11.4 %collective-permute-done.8 = bf16[16,256,128]{2,1,0:T(8,128)(2,1)S(1)} collective-permute-done((bf16[16,256,128]{2,1,0:T(8,128)(2,1)}, bf16[16,256,128]{2,1,0:T(8,128)(2,1)S(1)}, u32[]{:S(2)}, u32[]{:S(2)}) %collective-permute-start.8) | collective-permute-done | bytes 1048608 | tf_op jit(solution)/shard_map/ppermute | solution.py:39
  54.0 10.8 %collective-permute-done.2 = bf16[16,256,128]{2,1,0:T(8,128)(2,1)S(1)} collective-permute-done((bf16[16,256,128]{2,1,0:T(8,128)(2,1)S(1)}, bf16[16,256,128]{2,1,0:T(8,128)(2,1)S(1)}, u32[]{:S(2)}, u32[]{:S(2)}) %collective-permute-start.2) | collective-permute-done | bytes 1048608 | tf_op jit(solution)/shard_map/ppermute | solution.py:37
  67.2 12.2 %collective-permute-done.9 = bf16[16,256,128]{2,1,0:T(8,128)(2,1)S(1)} collective-permute-done((bf16[16,256,128]{2,1,0:T(8,128)(2,1)S(1)}, bf16[16,256,128]{2,1,0:T(8,128)(2,1)S(1)}, u32[]{:S(2)}, u32[]{:S(2)}) %collective-permute-start.9) | collective-permute-done | bytes 1048608 | tf_op jit(solution)/shard_map/ppermute | solution.py:39
  80.4 9.0 %collective-permute-done.3 = bf16[16,256,128]{2,1,0:T(8,128)(2,1)S(1)} collective-permute-done((bf16[16,256,128]{2,1,0:T(8,128)(2,1)S(1)}, bf16[16,256,128]{2,1,0:T(8,128)(2,1)S(1)}, u32[]{:S(2)}, u32[]{:S(2)}) %collective-permute-start.3) | collective-permute-done | bytes 1048608 | tf_op jit(solution)/shard_map/ppermute | solution.py:37
  92.0 11.6 %collective-permute-done.10 = bf16[16,256,128]{2,1,0:T(8,128)(2,1)S(1)} collective-permute-done((bf16[16,256,128]{2,1,0:T(8,128)(2,1)S(1)}, bf16[16,256,128]{2,1,0:T(8,128)(2,1)S(1)}, u32[]{:S(2)}, u32[]{:S(2)}) %collective-permute-start.10) | collective-permute-done | bytes 1048608 | tf_op jit(solution)/shard_map/ppermute | solution.py:39
  104.6 9.7 %collective-permute-done.4 = bf16[16,256,128]{2,1,0:T(8,128)(2,1)S(1)} collective-permute-done((bf16[16,256,128]{2,1,0:T(8,128)(2,1)S(1)}, bf16[16,256,128]{2,1,0:T(8,128)(2,1)S(1)}, u32[]{:S(2)}, u32[]{:S(2)}) %collective-permute-start.4) | collective-permute-done | bytes 1048608 | tf_op jit(solution)/shard_map/ppermute | solution.py:37
  116.7 10.2 %collective-permute-done.11 = bf16[16,256,128]{2,1,0:T(8,128)(2,1)S(1)} collective-permute-done((bf16[16,256,128]{2,1,0:T(8,128)(2,1)S(1)}, bf16[16,256,128]{2,1,0:T(8,128)(2,1)S(1)}, u32[]{:S(2)}, u32[]{:S(2)}) %collective-permute-start.11) | collective-permute-done | bytes 1048608 | tf_op jit(solution)/shard_map/ppermute | solution.py:39
  127.9 10.6 %collective-permute-done.5 = bf16[16,256,128]{2,1,0:T(8,128)(2,1)S(1)} collective-permute-done((bf16[16,256,128]{2,1,0:T(8,128)(2,1)S(1)}, bf16[16,256,128]{2,1,0:T(8,128)(2,1)S(1)}, u32[]{:S(2)}, u32[]{:S(2)}) %collective-permute-start.5) | collective-permute-done | bytes 1048608 | tf_op jit(solution)/shard_map/ppermute | solution.py:37
  141.0 10.5 %collective-permute-done.12 = bf16[16,256,128]{2,1,0:T(8,128)(2,1)} collective-permute-done((bf16[16,256,128]{2,1,0:T(8,128)(2,1)S(1)}, bf16[16,256,128]{2,1,0:T(8,128)(2,1)}, u32[]{:S(2)}, u32[]{:S(2)}) %collective-permute-start.12) | collective-permute-done | bytes 1048608 | tf_op jit(solution)/shard_map/ppermute | solution.py:39
  151.5 11.7 %collective-permute-done.6 = bf16[16,256,128]{2,1,0:T(8,128)(2,1)} collective-permute-done((bf16[16,256,128]{2,1,0:T(8,128)(2,1)S(1)}, bf16[16,256,128]{2,1,0:T(8,128)(2,1)}, u32[]{:S(2)}, u32[]{:S(2)}) %collective-permute-start.6) | collective-permute-done | bytes 1048608 | tf_op jit(solution)/shard_map/ppermute | solution.py:37
  177.1 12.0 %collective-permute-done.7 = bf16[16,256,128]{2,1,0:T(8,128)(2,1)} collective-permute-done((bf16[16,256,128]{2,1,0:T(8,128)(2,1)}, bf16[16,256,128]{2,1,0:T(8,128)(2,1)}, u32[]{:S(2)}, u32[]{:S(2)}) %collective-permute-start.7) | collective-permute-done | bytes 1048608 | tf_op jit(solution)/shard_map/ppermute | solution.py:37
  217.7 13.1 %gather_fusion.2 = bf16[16,16,256,128]{3,2,1,0:T(8,128)(2,1)} fusion(bf16[16,16,256,128]{3,2,1,0:T(8,128)(2,1)} %bitcast_dynamic-update-slice_fusion, s32[1024]{0:T(1024)S(1)} %pad_clamp_fusion.1), kind=kCustom, calls=%fused_computation.2 | custom fusion | bytes 33554496 | tf_op jit(solution)/shard_map/gather | solution.py:42
  230.8 575.8 %while.10 = (s32[]{:T(128)}, bf16[16,256,128]{2,1,0:T(8,128)(2,1)S(1)}, s32[16,64]{1,0:T(8,128)}, bf16[16,256,128]{2,1,0:T(8,128)(2,1)}, s32[16,64]{1,0:T(8,128)S(1)}, /*index=5*/bf16[256,256,128]{2,1,0:T(8,128)(2,1)}, s32[]{:T(128)}) while((s32[]{:T(128)}, bf16[16,256,128]{2,1,0:T(8,128)(2,1)S(1)}, s32[16,64]{1,0:T(8,128)}, ...), condition=%wide.region_3.4_spmd, body=%wide.region_0.3_spmd.sunk | while | flops 2181071616 | bytes 84093936 | solution.py:50
  230.8 8.9 %gather_fusion = bf16[64,256,128]{2,1,0:T(8,128)(2,1)} fusion(bf16[256,256,128]{2,1,0:T(8,128)(2,1)} %get-tuple-element.112, s32[1024]{0:T(1024)S(1)} %pad_clamp_fusion.3), kind=kCustom, calls=%fused_computation.clone.1 | custom fusion | bytes 8388864 | tf_op jit(solution)/shard_map/while/body/eval_jaxpr/gather | solution.py:47
  240.5 10.5 %fusion.25 = (f32[256]{0:T(256)S(1)}, f32[256,16384]{1,0:T(8,128)}) fusion(bf16[16384,128]{1,0:T(8,128)(2,1)} %bitcast.73, bf16[16,256,128]{2,1,0:T(8,128)(2,1)} %get-tuple-element.110, s32[]{:T(128)} %get-tuple-element.100, pred[16384]{0:T(1024)(128)(4,1)S(1)} %broadcast_in_dim.38), kind=kOutput, calls=%fused_computation.47.clone.1 | convolution fusion | flops 1086324480 | bytes 21054976 | tf_op jit(solution)/shard_map/while/body/eval_jaxpr/dot_general | solution.py:16
  251.0 8.1 %fusion.26 = f32[256]{0:T(256)S(1)} fusion(f32[256,16384]{1,0:T(8,128)} %get-tuple-element.91, f32[256]{0:T(256)S(1)} %get-tuple-element.92), kind=kLoop, calls=%fused_computation.7.clone.1 | loop fusion | flops 8388352 | bytes 16779264 | tf_op jit(solution)/shard_map/while/body/eval_jaxpr/reduce_sum | solution.py:23
  266.8 8.9 %gather_fusion = bf16[64,256,128]{2,1,0:T(8,128)(2,1)} fusion(bf16[256,256,128]{2,1,0:T(8,128)(2,1)} %get-tuple-element.112, s32[1024]{0:T(1024)S(1)} %pad_clamp_fusion.3), kind=kCustom, calls=%fused_computation.clone.1 | custom fusion | bytes 8388864 | tf_op jit(solution)/shard_map/while/body/eval_jaxpr/gather | solution.py:47
  276.5 10.5 %fusion.25 = (f32[256]{0:T(256)S(1)}, f32[256,16384]{1,0:T(8,128)}) fusion(bf16[16384,128]{1,0:T(8,128)(2,1)} %bitcast.73, bf16[16,256,128]{2,1,0:T(8,128)(2,1)} %get-tuple-element.110, s32[]{:T(128)} %get-tuple-element.100, pred[16384]{0:T(1024)(128)(4,1)S(1)} %broadcast_in_dim.38), kind=kOutput, calls=%fused_computation.47.clone.1 | convolution fusion | flops 1086324480 | bytes 21054976 | tf_op jit(solution)/shard_map/while/body/eval_jaxpr/dot_general | solution.py:16
  287.0 8.1 %fusion.26 = f32[256]{0:T(256)S(1)} fusion(f32[256,16384]{1,0:T(8,128)} %get-tuple-element.91, f32[256]{0:T(256)S(1)} %get-tuple-element.92), kind=kLoop, calls=%fused_computation.7.clone.1 | loop fusion | flops 8388352 | bytes 16779264 | tf_op jit(solution)/shard_map/while/body/eval_jaxpr/reduce_sum | solution.py:23
  295.1 7.6 fusion.27
  302.8 8.9 %gather_fusion = bf16[64,256,128]{2,1,0:T(8,128)(2,1)} fusion(bf16[256,256,128]{2,1,0:T(8,128)(2,1)} %get-tuple-element.112, s32[1024]{0:T(1024)S(1)} %pad_clamp_fusion.3), kind=kCustom, calls=%fused_computation.clone.1 | custom fusion | bytes 8388864 | tf_op jit(solution)/shard_map/while/body/eval_jaxpr/gather | solution.py:47
  312.5 10.5 %fusion.25 = (f32[256]{0:T(256)S(1)}, f32[256,16384]{1,0:T(8,128)}) fusion(bf16[16384,128]{1,0:T(8,128)(2,1)} %bitcast.73, bf16[16,256,128]{2,1,0:T(8,128)(2,1)} %get-tuple-element.110, s32[]{:T(128)} %get-tuple-element.100, pred[16384]{0:T(1024)(128)(4,1)S(1)} %broadcast_in_dim.38), kind=kOutput, calls=%fused_computation.47.clone.1 | convolution fusion | flops 1086324480 | bytes 21054976 | tf_op jit(solution)/shard_map/while/body/eval_jaxpr/dot_general | solution.py:16
  323.0 8.1 %fusion.26 = f32[256]{0:T(256)S(1)} fusion(f32[256,16384]{1,0:T(8,128)} %get-tuple-element.91, f32[256]{0:T(256)S(1)} %get-tuple-element.92), kind=kLoop, calls=%fused_computation.7.clone.1 | loop fusion | flops 8388352 | bytes 16779264 | tf_op jit(solution)/shard_map/while/body/eval_jaxpr/reduce_sum | solution.py:23
  338.8 8.9 %gather_fusion = bf16[64,256,128]{2,1,0:T(8,128)(2,1)} fusion(bf16[256,256,128]{2,1,0:T(8,128)(2,1)} %get-tuple-element.112, s32[1024]{0:T(1024)S(1)} %pad_clamp_fusion.3), kind=kCustom, calls=%fused_computation.clone.1 | custom fusion | bytes 8388864 | tf_op jit(solution)/shard_map/while/body/eval_jaxpr/gather | solution.py:47
  348.5 10.5 %fusion.25 = (f32[256]{0:T(256)S(1)}, f32[256,16384]{1,0:T(8,128)}) fusion(bf16[16384,128]{1,0:T(8,128)(2,1)} %bitcast.73, bf16[16,256,128]{2,1,0:T(8,128)(2,1)} %get-tuple-element.110, s32[]{:T(128)} %get-tuple-element.100, pred[16384]{0:T(1024)(128)(4,1)S(1)} %broadcast_in_dim.38), kind=kOutput, calls=%fused_computation.47.clone.1 | convolution fusion | flops 1086324480 | bytes 21054976 | tf_op jit(solution)/shard_map/while/body/eval_jaxpr/dot_general | solution.py:16
  359.0 8.1 %fusion.26 = f32[256]{0:T(256)S(1)} fusion(f32[256,16384]{1,0:T(8,128)} %get-tuple-element.91, f32[256]{0:T(256)S(1)} %get-tuple-element.92), kind=kLoop, calls=%fused_computation.7.clone.1 | loop fusion | flops 8388352 | bytes 16779264 | tf_op jit(solution)/shard_map/while/body/eval_jaxpr/reduce_sum | solution.py:23
  374.8 8.9 %gather_fusion = bf16[64,256,128]{2,1,0:T(8,128)(2,1)} fusion(bf16[256,256,128]{2,1,0:T(8,128)(2,1)} %get-tuple-element.112, s32[1024]{0:T(1024)S(1)} %pad_clamp_fusion.3), kind=kCustom, calls=%fused_computation.clone.1 | custom fusion | bytes 8388864 | tf_op jit(solution)/shard_map/while/body/eval_jaxpr/gather | solution.py:47
  384.5 10.5 %fusion.25 = (f32[256]{0:T(256)S(1)}, f32[256,16384]{1,0:T(8,128)}) fusion(bf16[16384,128]{1,0:T(8,128)(2,1)} %bitcast.73, bf16[16,256,128]{2,1,0:T(8,128)(2,1)} %get-tuple-element.110, s32[]{:T(128)} %get-tuple-element.100, pred[16384]{0:T(1024)(128)(4,1)S(1)} %broadcast_in_dim.38), kind=kOutput, calls=%fused_computation.47.clone.1 | convolution fusion | flops 1086324480 | bytes 21054976 | tf_op jit(solution)/shard_map/while/body/eval_jaxpr/dot_general | solution.py:16
  394.9 8.1 %fusion.26 = f32[256]{0:T(256)S(1)} fusion(f32[256,16384]{1,0:T(8,128)} %get-tuple-element.91, f32[256]{0:T(256)S(1)} %get-tuple-element.92), kind=kLoop, calls=%fused_computation.7.clone.1 | loop fusion | flops 8388352 | bytes 16779264 | tf_op jit(solution)/shard_map/while/body/eval_jaxpr/reduce_sum | solution.py:23
  410.8 8.9 %gather_fusion = bf16[64,256,128]{2,1,0:T(8,128)(2,1)} fusion(bf16[256,256,128]{2,1,0:T(8,128)(2,1)} %get-tuple-element.112, s32[1024]{0:T(1024)S(1)} %pad_clamp_fusion.3), kind=kCustom, calls=%fused_computation.clone.1 | custom fusion | bytes 8388864 | tf_op jit(solution)/shard_map/while/body/eval_jaxpr/gather | solution.py:47
  420.5 10.5 %fusion.25 = (f32[256]{0:T(256)S(1)}, f32[256,16384]{1,0:T(8,128)}) fusion(bf16[16384,128]{1,0:T(8,128)(2,1)} %bitcast.73, bf16[16,256,128]{2,1,0:T(8,128)(2,1)} %get-tuple-element.110, s32[]{:T(128)} %get-tuple-element.100, pred[16384]{0:T(1024)(128)(4,1)S(1)} %broadcast_in_dim.38), kind=kOutput, calls=%fused_computation.47.clone.1 | convolution fusion | flops 1086324480 | bytes 21054976 | tf_op jit(solution)/shard_map/while/body/eval_jaxpr/dot_general | solution.py:16
  430.9 8.1 %fusion.26 = f32[256]{0:T(256)S(1)} fusion(f32[256,16384]{1,0:T(8,128)} %get-tuple-element.91, f32[256]{0:T(256)S(1)} %get-tuple-element.92), kind=kLoop, calls=%fused_computation.7.clone.1 | loop fusion | flops 8388352 | bytes 16779264 | tf_op jit(solution)/shard_map/while/body/eval_jaxpr/reduce_sum | solution.py:23
  446.7 8.9 %gather_fusion = bf16[64,256,128]{2,1,0:T(8,128)(2,1)} fusion(bf16[256,256,128]{2,1,0:T(8,128)(2,1)} %get-tuple-element.112, s32[1024]{0:T(1024)S(1)} %pad_clamp_fusion.3), kind=kCustom, calls=%fused_computation.clone.1 | custom fusion | bytes 8388864 | tf_op jit(solution)/shard_map/while/body/eval_jaxpr/gather | solution.py:47
  456.5 10.5 %fusion.25 = (f32[256]{0:T(256)S(1)}, f32[256,16384]{1,0:T(8,128)}) fusion(bf16[16384,128]{1,0:T(8,128)(2,1)} %bitcast.73, bf16[16,256,128]{2,1,0:T(8,128)(2,1)} %get-tuple-element.110, s32[]{:T(128)} %get-tuple-element.100, pred[16384]{0:T(1024)(128)(4,1)S(1)} %broadcast_in_dim.38), kind=kOutput, calls=%fused_computation.47.clone.1 | convolution fusion | flops 1086324480 | bytes 21054976 | tf_op jit(solution)/shard_map/while/body/eval_jaxpr/dot_general | solution.py:16
  466.9 8.1 %fusion.26 = f32[256]{0:T(256)S(1)} fusion(f32[256,16384]{1,0:T(8,128)} %get-tuple-element.91, f32[256]{0:T(256)S(1)} %get-tuple-element.92), kind=kLoop, calls=%fused_computation.7.clone.1 | loop fusion | flops 8388352 | bytes 16779264 | tf_op jit(solution)/shard_map/while/body/eval_jaxpr/reduce_sum | solution.py:23
  482.7 8.9 %gather_fusion = bf16[64,256,128]{2,1,0:T(8,128)(2,1)} fusion(bf16[256,256,128]{2,1,0:T(8,128)(2,1)} %get-tuple-element.112, s32[1024]{0:T(1024)S(1)} %pad_clamp_fusion.3), kind=kCustom, calls=%fused_computation.clone.1 | custom fusion | bytes 8388864 | tf_op jit(solution)/shard_map/while/body/eval_jaxpr/gather | solution.py:47
  492.5 10.5 %fusion.25 = (f32[256]{0:T(256)S(1)}, f32[256,16384]{1,0:T(8,128)}) fusion(bf16[16384,128]{1,0:T(8,128)(2,1)} %bitcast.73, bf16[16,256,128]{2,1,0:T(8,128)(2,1)} %get-tuple-element.110, s32[]{:T(128)} %get-tuple-element.100, pred[16384]{0:T(1024)(128)(4,1)S(1)} %broadcast_in_dim.38), kind=kOutput, calls=%fused_computation.47.clone.1 | convolution fusion | flops 1086324480 | bytes 21054976 | tf_op jit(solution)/shard_map/while/body/eval_jaxpr/dot_general | solution.py:16
  502.9 8.1 %fusion.26 = f32[256]{0:T(256)S(1)} fusion(f32[256,16384]{1,0:T(8,128)} %get-tuple-element.91, f32[256]{0:T(256)S(1)} %get-tuple-element.92), kind=kLoop, calls=%fused_computation.7.clone.1 | loop fusion | flops 8388352 | bytes 16779264 | tf_op jit(solution)/shard_map/while/body/eval_jaxpr/reduce_sum | solution.py:23
  518.7 8.9 %gather_fusion = bf16[64,256,128]{2,1,0:T(8,128)(2,1)} fusion(bf16[256,256,128]{2,1,0:T(8,128)(2,1)} %get-tuple-element.112, s32[1024]{0:T(1024)S(1)} %pad_clamp_fusion.3), kind=kCustom, calls=%fused_computation.clone.1 | custom fusion | bytes 8388864 | tf_op jit(solution)/shard_map/while/body/eval_jaxpr/gather | solution.py:47
  528.5 10.5 %fusion.25 = (f32[256]{0:T(256)S(1)}, f32[256,16384]{1,0:T(8,128)}) fusion(bf16[16384,128]{1,0:T(8,128)(2,1)} %bitcast.73, bf16[16,256,128]{2,1,0:T(8,128)(2,1)} %get-tuple-element.110, s32[]{:T(128)} %get-tuple-element.100, pred[16384]{0:T(1024)(128)(4,1)S(1)} %broadcast_in_dim.38), kind=kOutput, calls=%fused_computation.47.clone.1 | convolution fusion | flops 1086324480 | bytes 21054976 | tf_op jit(solution)/shard_map/while/body/eval_jaxpr/dot_general | solution.py:16
  538.9 8.1 %fusion.26 = f32[256]{0:T(256)S(1)} fusion(f32[256,16384]{1,0:T(8,128)} %get-tuple-element.91, f32[256]{0:T(256)S(1)} %get-tuple-element.92), kind=kLoop, calls=%fused_computation.7.clone.1 | loop fusion | flops 8388352 | bytes 16779264 | tf_op jit(solution)/shard_map/while/body/eval_jaxpr/reduce_sum | solution.py:23
  554.7 8.9 %gather_fusion = bf16[64,256,128]{2,1,0:T(8,128)(2,1)} fusion(bf16[256,256,128]{2,1,0:T(8,128)(2,1)} %get-tuple-element.112, s32[1024]{0:T(1024)S(1)} %pad_clamp_fusion.3), kind=kCustom, calls=%fused_computation.clone.1 | custom fusion | bytes 8388864 | tf_op jit(solution)/shard_map/while/body/eval_jaxpr/gather | solution.py:47
  564.5 10.5 %fusion.25 = (f32[256]{0:T(256)S(1)}, f32[256,16384]{1,0:T(8,128)}) fusion(bf16[16384,128]{1,0:T(8,128)(2,1)} %bitcast.73, bf16[16,256,128]{2,1,0:T(8,128)(2,1)} %get-tuple-element.110, s32[]{:T(128)} %get-tuple-element.100, pred[16384]{0:T(1024)(128)(4,1)S(1)} %broadcast_in_dim.38), kind=kOutput, calls=%fused_computation.47.clone.1 | convolution fusion | flops 1086324480 | bytes 21054976 | tf_op jit(solution)/shard_map/while/body/eval_jaxpr/dot_general | solution.py:16
  574.9 8.1 %fusion.26 = f32[256]{0:T(256)S(1)} fusion(f32[256,16384]{1,0:T(8,128)} %get-tuple-element.91, f32[256]{0:T(256)S(1)} %get-tuple-element.92), kind=kLoop, calls=%fused_computation.7.clone.1 | loop fusion | flops 8388352 | bytes 16779264 | tf_op jit(solution)/shard_map/while/body/eval_jaxpr/reduce_sum | solution.py:23
  590.7 8.9 %gather_fusion = bf16[64,256,128]{2,1,0:T(8,128)(2,1)} fusion(bf16[256,256,128]{2,1,0:T(8,128)(2,1)} %get-tuple-element.112, s32[1024]{0:T(1024)S(1)} %pad_clamp_fusion.3), kind=kCustom, calls=%fused_computation.clone.1 | custom fusion | bytes 8388864 | tf_op jit(solution)/shard_map/while/body/eval_jaxpr/gather | solution.py:47
  600.4 10.5 %fusion.25 = (f32[256]{0:T(256)S(1)}, f32[256,16384]{1,0:T(8,128)}) fusion(bf16[16384,128]{1,0:T(8,128)(2,1)} %bitcast.73, bf16[16,256,128]{2,1,0:T(8,128)(2,1)} %get-tuple-element.110, s32[]{:T(128)} %get-tuple-element.100, pred[16384]{0:T(1024)(128)(4,1)S(1)} %broadcast_in_dim.38), kind=kOutput, calls=%fused_computation.47.clone.1 | convolution fusion | flops 1086324480 | bytes 21054976 | tf_op jit(solution)/shard_map/while/body/eval_jaxpr/dot_general | solution.py:16
  610.9 8.1 %fusion.26 = f32[256]{0:T(256)S(1)} fusion(f32[256,16384]{1,0:T(8,128)} %get-tuple-element.91, f32[256]{0:T(256)S(1)} %get-tuple-element.92), kind=kLoop, calls=%fused_computation.7.clone.1 | loop fusion | flops 8388352 | bytes 16779264 | tf_op jit(solution)/shard_map/while/body/eval_jaxpr/reduce_sum | solution.py:23
  626.7 8.9 %gather_fusion = bf16[64,256,128]{2,1,0:T(8,128)(2,1)} fusion(bf16[256,256,128]{2,1,0:T(8,128)(2,1)} %get-tuple-element.112, s32[1024]{0:T(1024)S(1)} %pad_clamp_fusion.3), kind=kCustom, calls=%fused_computation.clone.1 | custom fusion | bytes 8388864 | tf_op jit(solution)/shard_map/while/body/eval_jaxpr/gather | solution.py:47
  636.4 10.5 %fusion.25 = (f32[256]{0:T(256)S(1)}, f32[256,16384]{1,0:T(8,128)}) fusion(bf16[16384,128]{1,0:T(8,128)(2,1)} %bitcast.73, bf16[16,256,128]{2,1,0:T(8,128)(2,1)} %get-tuple-element.110, s32[]{:T(128)} %get-tuple-element.100, pred[16384]{0:T(1024)(128)(4,1)S(1)} %broadcast_in_dim.38), kind=kOutput, calls=%fused_computation.47.clone.1 | convolution fusion | flops 1086324480 | bytes 21054976 | tf_op jit(solution)/shard_map/while/body/eval_jaxpr/dot_general | solution.py:16
  646.9 8.1 %fusion.26 = f32[256]{0:T(256)S(1)} fusion(f32[256,16384]{1,0:T(8,128)} %get-tuple-element.91, f32[256]{0:T(256)S(1)} %get-tuple-element.92), kind=kLoop, calls=%fused_computation.7.clone.1 | loop fusion | flops 8388352 | bytes 16779264 | tf_op jit(solution)/shard_map/while/body/eval_jaxpr/reduce_sum | solution.py:23
  662.7 8.9 %gather_fusion = bf16[64,256,128]{2,1,0:T(8,128)(2,1)} fusion(bf16[256,256,128]{2,1,0:T(8,128)(2,1)} %get-tuple-element.112, s32[1024]{0:T(1024)S(1)} %pad_clamp_fusion.3), kind=kCustom, calls=%fused_computation.clone.1 | custom fusion | bytes 8388864 | tf_op jit(solution)/shard_map/while/body/eval_jaxpr/gather | solution.py:47
  672.4 10.5 %fusion.25 = (f32[256]{0:T(256)S(1)}, f32[256,16384]{1,0:T(8,128)}) fusion(bf16[16384,128]{1,0:T(8,128)(2,1)} %bitcast.73, bf16[16,256,128]{2,1,0:T(8,128)(2,1)} %get-tuple-element.110, s32[]{:T(128)} %get-tuple-element.100, pred[16384]{0:T(1024)(128)(4,1)S(1)} %broadcast_in_dim.38), kind=kOutput, calls=%fused_computation.47.clone.1 | convolution fusion | flops 1086324480 | bytes 21054976 | tf_op jit(solution)/shard_map/while/body/eval_jaxpr/dot_general | solution.py:16
  682.9 8.1 %fusion.26 = f32[256]{0:T(256)S(1)} fusion(f32[256,16384]{1,0:T(8,128)} %get-tuple-element.91, f32[256]{0:T(256)S(1)} %get-tuple-element.92), kind=kLoop, calls=%fused_computation.7.clone.1 | loop fusion | flops 8388352 | bytes 16779264 | tf_op jit(solution)/shard_map/while/body/eval_jaxpr/reduce_sum | solution.py:23
  698.7 8.9 %gather_fusion = bf16[64,256,128]{2,1,0:T(8,128)(2,1)} fusion(bf16[256,256,128]{2,1,0:T(8,128)(2,1)} %get-tuple-element.112, s32[1024]{0:T(1024)S(1)} %pad_clamp_fusion.3), kind=kCustom, calls=%fused_computation.clone.1 | custom fusion | bytes 8388864 | tf_op jit(solution)/shard_map/while/body/eval_jaxpr/gather | solution.py:47
  708.4 10.5 %fusion.25 = (f32[256]{0:T(256)S(1)}, f32[256,16384]{1,0:T(8,128)}) fusion(bf16[16384,128]{1,0:T(8,128)(2,1)} %bitcast.73, bf16[16,256,128]{2,1,0:T(8,128)(2,1)} %get-tuple-element.110, s32[]{:T(128)} %get-tuple-element.100, pred[16384]{0:T(1024)(128)(4,1)S(1)} %broadcast_in_dim.38), kind=kOutput, calls=%fused_computation.47.clone.1 | convolution fusion | flops 1086324480 | bytes 21054976 | tf_op jit(solution)/shard_map/while/body/eval_jaxpr/dot_general | solution.py:16
  718.9 8.1 %fusion.26 = f32[256]{0:T(256)S(1)} fusion(f32[256,16384]{1,0:T(8,128)} %get-tuple-element.91, f32[256]{0:T(256)S(1)} %get-tuple-element.92), kind=kLoop, calls=%fused_computation.7.clone.1 | loop fusion | flops 8388352 | bytes 16779264 | tf_op jit(solution)/shard_map/while/body/eval_jaxpr/reduce_sum | solution.py:23
  734.7 8.9 %gather_fusion = bf16[64,256,128]{2,1,0:T(8,128)(2,1)} fusion(bf16[256,256,128]{2,1,0:T(8,128)(2,1)} %get-tuple-element.112, s32[1024]{0:T(1024)S(1)} %pad_clamp_fusion.3), kind=kCustom, calls=%fused_computation.clone.1 | custom fusion | bytes 8388864 | tf_op jit(solution)/shard_map/while/body/eval_jaxpr/gather | solution.py:47
  744.4 10.5 %fusion.25 = (f32[256]{0:T(256)S(1)}, f32[256,16384]{1,0:T(8,128)}) fusion(bf16[16384,128]{1,0:T(8,128)(2,1)} %bitcast.73, bf16[16,256,128]{2,1,0:T(8,128)(2,1)} %get-tuple-element.110, s32[]{:T(128)} %get-tuple-element.100, pred[16384]{0:T(1024)(128)(4,1)S(1)} %broadcast_in_dim.38), kind=kOutput, calls=%fused_computation.47.clone.1 | convolution fusion | flops 1086324480 | bytes 21054976 | tf_op jit(solution)/shard_map/while/body/eval_jaxpr/dot_general | solution.py:16
  754.9 8.1 %fusion.26 = f32[256]{0:T(256)S(1)} fusion(f32[256,16384]{1,0:T(8,128)} %get-tuple-element.91, f32[256]{0:T(256)S(1)} %get-tuple-element.92), kind=kLoop, calls=%fused_computation.7.clone.1 | loop fusion | flops 8388352 | bytes 16779264 | tf_op jit(solution)/shard_map/while/body/eval_jaxpr/reduce_sum | solution.py:23
  770.7 8.9 %gather_fusion = bf16[64,256,128]{2,1,0:T(8,128)(2,1)} fusion(bf16[256,256,128]{2,1,0:T(8,128)(2,1)} %get-tuple-element.112, s32[1024]{0:T(1024)S(1)} %pad_clamp_fusion.3), kind=kCustom, calls=%fused_computation.clone.1 | custom fusion | bytes 8388864 | tf_op jit(solution)/shard_map/while/body/eval_jaxpr/gather | solution.py:47
  780.4 10.5 %fusion.25 = (f32[256]{0:T(256)S(1)}, f32[256,16384]{1,0:T(8,128)}) fusion(bf16[16384,128]{1,0:T(8,128)(2,1)} %bitcast.73, bf16[16,256,128]{2,1,0:T(8,128)(2,1)} %get-tuple-element.110, s32[]{:T(128)} %get-tuple-element.100, pred[16384]{0:T(1024)(128)(4,1)S(1)} %broadcast_in_dim.38), kind=kOutput, calls=%fused_computation.47.clone.1 | convolution fusion | flops 1086324480 | bytes 21054976 | tf_op jit(solution)/shard_map/while/body/eval_jaxpr/dot_general | solution.py:16
  790.9 8.1 %fusion.26 = f32[256]{0:T(256)S(1)} fusion(f32[256,16384]{1,0:T(8,128)} %get-tuple-element.91, f32[256]{0:T(256)S(1)} %get-tuple-element.92), kind=kLoop, calls=%fused_computation.7.clone.1 | loop fusion | flops 8388352 | bytes 16779264 | tf_op jit(solution)/shard_map/while/body/eval_jaxpr/reduce_sum | solution.py:23
  (200 shorter events, 192.6 us)
Async XLA Ops:
  0.0 166.6 %copy-start = (s32[256]{0:T(256)S(1)}, s32[256]{0:T(256)}, u32[]{:S(2)}) copy-start(s32[256]{0:T(256)} %param.9) | copy-start | bytes 3076
  0.0 206.5 %copy-start.3 = (bf16[16,256,128]{2,1,0:T(8,128)(2,1)S(1)}, bf16[16,256,128]{2,1,0:T(8,128)(2,1)}, u32[]{:S(2)}) copy-start(bf16[16,256,128]{2,1,0:T(8,128)(2,1)} %param.8) | copy-start | bytes 3145732
  0.0 14.7 %collective-permute-start = (bf16[16,256,128]{2,1,0:T(8,128)(2,1)}, bf16[16,256,128]{2,1,0:T(8,128)(2,1)S(1)}, u32[]{:S(2)}, u32[]{:S(2)}) collective-permute-start(bf16[16,256,128]{2,1,0:T(8,128)(2,1)} %param.8), channel_id=1, source_target_pairs={{0,1},{1,2},{2,3},{3,4},{4,5},{5,6},{6,7},{7,8},{8,9},{9,10},{10,1... | collective-permute-start | bytes 3145736 | tf_op jit(solution)/shard_map/ppermute | solution.py:37
  14.7 25.4 %collective-permute-start.1 = (bf16[16,256,128]{2,1,0:T(8,128)(2,1)S(1)}, bf16[16,256,128]{2,1,0:T(8,128)(2,1)S(1)}, u32[]{:S(2)}, u32[]{:S(2)}) collective-permute-start(bf16[16,256,128]{2,1,0:T(8,128)(2,1)S(1)} %collective-permute-done), channel_id=1, source_target_pairs={{0,1},{1,2},{2,3},{3,4},{4,5},{5,6},{6,7},{7,8},{8,9},{9,10},{10,1... | collective-permute-start | bytes 3145736 | tf_op jit(solution)/shard_map/ppermute | solution.py:37
  17.1 36.9 %collective-permute-start.8 = (bf16[16,256,128]{2,1,0:T(8,128)(2,1)}, bf16[16,256,128]{2,1,0:T(8,128)(2,1)S(1)}, u32[]{:S(2)}, u32[]{:S(2)}) collective-permute-start(bf16[16,256,128]{2,1,0:T(8,128)(2,1)} %param.8), channel_id=1, source_target_pairs={{1,0},{2,1},{3,2},{4,3},{5,4},{6,5},{7,6},{8,7},{9,8},{10,9},{11,1... | collective-permute-start | bytes 3145736 | tf_op jit(solution)/shard_map/ppermute | solution.py:39
  40.0 39.4 %copy-start.4 = (bf16[16,256,128]{2,1,0:T(8,128)(2,1)}, bf16[16,256,128]{2,1,0:T(8,128)(2,1)S(1)}, u32[]{:S(2)}) copy-start(bf16[16,256,128]{2,1,0:T(8,128)(2,1)S(1)} %collective-permute-done.1) | copy-start | bytes 3145732
  40.0 24.7 %collective-permute-start.2 = (bf16[16,256,128]{2,1,0:T(8,128)(2,1)S(1)}, bf16[16,256,128]{2,1,0:T(8,128)(2,1)S(1)}, u32[]{:S(2)}, u32[]{:S(2)}) collective-permute-start(bf16[16,256,128]{2,1,0:T(8,128)(2,1)S(1)} %collective-permute-done.1), channel_id=1, source_target_pairs={{0,1},{1,2},{2,3},{3,4},{4,5},{5,6},{6,7},{7,8},{8,9},{9,10},{10,1... | collective-permute-start | bytes 3145736 | tf_op jit(solution)/shard_map/ppermute | solution.py:37
  54.0 25.5 %collective-permute-start.9 = (bf16[16,256,128]{2,1,0:T(8,128)(2,1)S(1)}, bf16[16,256,128]{2,1,0:T(8,128)(2,1)S(1)}, u32[]{:S(2)}, u32[]{:S(2)}) collective-permute-start(bf16[16,256,128]{2,1,0:T(8,128)(2,1)S(1)} %collective-permute-done.8), channel_id=1, source_target_pairs={{1,0},{2,1},{3,2},{4,3},{5,4},{6,5},{7,6},{8,7},{9,8},{10,9},{11,1... | collective-permute-start | bytes 3145736 | tf_op jit(solution)/shard_map/ppermute | solution.py:39
  64.7 38.9 %copy-start.7 = (bf16[16,256,128]{2,1,0:T(8,128)(2,1)}, bf16[16,256,128]{2,1,0:T(8,128)(2,1)S(1)}, u32[]{:S(2)}) copy-start(bf16[16,256,128]{2,1,0:T(8,128)(2,1)S(1)} %collective-permute-done.2) | copy-start | bytes 3145732
  64.7 24.7 %collective-permute-start.3 = (bf16[16,256,128]{2,1,0:T(8,128)(2,1)S(1)}, bf16[16,256,128]{2,1,0:T(8,128)(2,1)S(1)}, u32[]{:S(2)}, u32[]{:S(2)}) collective-permute-start(bf16[16,256,128]{2,1,0:T(8,128)(2,1)S(1)} %collective-permute-done.2), channel_id=1, source_target_pairs={{0,1},{1,2},{2,3},{3,4},{4,5},{5,6},{6,7},{7,8},{8,9},{9,10},{10,1... | collective-permute-start | bytes 3145736 | tf_op jit(solution)/shard_map/ppermute | solution.py:37
  79.4 1.0 copy-start.5
  79.4 24.2 %collective-permute-start.10 = (bf16[16,256,128]{2,1,0:T(8,128)(2,1)S(1)}, bf16[16,256,128]{2,1,0:T(8,128)(2,1)S(1)}, u32[]{:S(2)}, u32[]{:S(2)}) collective-permute-start(bf16[16,256,128]{2,1,0:T(8,128)(2,1)S(1)} %collective-permute-done.9), channel_id=1, source_target_pairs={{1,0},{2,1},{3,2},{4,3},{5,4},{6,5},{7,6},{8,7},{9,8},{10,9},{11,1... | collective-permute-start | bytes 3145736 | tf_op jit(solution)/shard_map/ppermute | solution.py:39
  89.5 62.0 %copy-start.12 = (bf16[16,256,128]{2,1,0:T(8,128)(2,1)}, bf16[16,256,128]{2,1,0:T(8,128)(2,1)S(1)}, u32[]{:S(2)}) copy-start(bf16[16,256,128]{2,1,0:T(8,128)(2,1)S(1)} %collective-permute-done.3) | copy-start | bytes 3145732
  89.5 24.7 %collective-permute-start.4 = (bf16[16,256,128]{2,1,0:T(8,128)(2,1)S(1)}, bf16[16,256,128]{2,1,0:T(8,128)(2,1)S(1)}, u32[]{:S(2)}, u32[]{:S(2)}) collective-permute-start(bf16[16,256,128]{2,1,0:T(8,128)(2,1)S(1)} %collective-permute-done.3), channel_id=1, source_target_pairs={{0,1},{1,2},{2,3},{3,4},{4,5},{5,6},{6,7},{7,8},{8,9},{9,10},{10,1... | collective-permute-start | bytes 3145736 | tf_op jit(solution)/shard_map/ppermute | solution.py:37
  103.6 1.0 copy-start.8
  103.6 23.3 %collective-permute-start.11 = (bf16[16,256,128]{2,1,0:T(8,128)(2,1)S(1)}, bf16[16,256,128]{2,1,0:T(8,128)(2,1)S(1)}, u32[]{:S(2)}, u32[]{:S(2)}) collective-permute-start(bf16[16,256,128]{2,1,0:T(8,128)(2,1)S(1)} %collective-permute-done.10), channel_id=1, source_target_pairs={{1,0},{2,1},{3,2},{4,3},{5,4},{6,5},{7,6},{8,7},{9,8},{10,9},{11,1... | collective-permute-start | bytes 3145736 | tf_op jit(solution)/shard_map/ppermute | solution.py:39
  114.2 37.3 %copy-start.13 = (bf16[16,256,128]{2,1,0:T(8,128)(2,1)}, bf16[16,256,128]{2,1,0:T(8,128)(2,1)S(1)}, u32[]{:S(2)}) copy-start(bf16[16,256,128]{2,1,0:T(8,128)(2,1)S(1)} %collective-permute-done.4) | copy-start | bytes 3145732
  114.2 24.3 %collective-permute-start.5 = (bf16[16,256,128]{2,1,0:T(8,128)(2,1)S(1)}, bf16[16,256,128]{2,1,0:T(8,128)(2,1)S(1)}, u32[]{:S(2)}, u32[]{:S(2)}) collective-permute-start(bf16[16,256,128]{2,1,0:T(8,128)(2,1)S(1)} %collective-permute-done.4), channel_id=1, source_target_pairs={{0,1},{1,2},{2,3},{3,4},{4,5},{5,6},{6,7},{7,8},{8,9},{9,10},{10,1... | collective-permute-start | bytes 3145736 | tf_op jit(solution)/shard_map/ppermute | solution.py:37
  126.9 1.0 copy-start.10
  127.9 23.6 %collective-permute-start.12 = (bf16[16,256,128]{2,1,0:T(8,128)(2,1)S(1)}, bf16[16,256,128]{2,1,0:T(8,128)(2,1)}, u32[]{:S(2)}, u32[]{:S(2)}) collective-permute-start(bf16[16,256,128]{2,1,0:T(8,128)(2,1)S(1)} %collective-permute-done.11), channel_id=1, source_target_pairs={{1,0},{2,1},{3,2},{4,3},{5,4},{6,5},{7,6},{8,7},{9,8},{10,9},{11,1... | collective-permute-start | bytes 3145736 | tf_op jit(solution)/shard_map/ppermute | solution.py:39
  138.6 24.7 %copy-start.14 = (bf16[16,256,128]{2,1,0:T(8,128)(2,1)}, bf16[16,256,128]{2,1,0:T(8,128)(2,1)S(1)}, u32[]{:S(2)}) copy-start(bf16[16,256,128]{2,1,0:T(8,128)(2,1)S(1)} %collective-permute-done.5) | copy-start | bytes 3145732
  138.6 24.7 %collective-permute-start.6 = (bf16[16,256,128]{2,1,0:T(8,128)(2,1)S(1)}, bf16[16,256,128]{2,1,0:T(8,128)(2,1)}, u32[]{:S(2)}, u32[]{:S(2)}) collective-permute-start(bf16[16,256,128]{2,1,0:T(8,128)(2,1)S(1)} %collective-permute-done.5), channel_id=1, source_target_pairs={{0,1},{1,2},{2,3},{3,4},{4,5},{5,6},{6,7},{7,8},{8,9},{9,10},{10,1... | collective-permute-start | bytes 3145736 | tf_op jit(solution)/shard_map/ppermute | solution.py:37
  151.5 25.6 %collective-permute-start.13 = (bf16[16,256,128]{2,1,0:T(8,128)(2,1)}, bf16[16,256,128]{2,1,0:T(8,128)(2,1)}, u32[]{:S(2)}, u32[]{:S(2)}) collective-permute-start(bf16[16,256,128]{2,1,0:T(8,128)(2,1)} %collective-permute-done.12), channel_id=1, source_target_pairs={{1,0},{2,1},{3,2},{4,3},{5,4},{6,5},{7,6},{8,7},{9,8},{10,9},{11,1... | collective-permute-start | bytes 3145736 | tf_op jit(solution)/shard_map/ppermute | solution.py:39
  163.2 25.9 %collective-permute-start.7 = (bf16[16,256,128]{2,1,0:T(8,128)(2,1)}, bf16[16,256,128]{2,1,0:T(8,128)(2,1)}, u32[]{:S(2)}, u32[]{:S(2)}) collective-permute-start(bf16[16,256,128]{2,1,0:T(8,128)(2,1)} %collective-permute-done.6), channel_id=1, source_target_pairs={{0,1},{1,2},{2,3},{3,4},{4,5},{5,6},{6,7},{7,8},{8,9},{9,10},{10,1... | collective-permute-start | bytes 3145736 | tf_op jit(solution)/shard_map/ppermute | solution.py:37
  173.5 35.2 %copy-start.6 = (bf16[16,256,128]{2,1,0:T(8,128)(2,1)S(1)}, bf16[16,256,128]{2,1,0:T(8,128)(2,1)}, u32[]{:S(2)}) copy-start(bf16[16,256,128]{2,1,0:T(8,128)(2,1)} %copy-done.5) | copy-start | bytes 3145732
  173.5 36.2 %copy-start.9 = (bf16[16,256,128]{2,1,0:T(8,128)(2,1)S(1)}, bf16[16,256,128]{2,1,0:T(8,128)(2,1)}, u32[]{:S(2)}) copy-start(bf16[16,256,128]{2,1,0:T(8,128)(2,1)} %copy-done.8) | copy-start | bytes 3145732
  173.5 37.3 %copy-start.11 = (bf16[16,256,128]{2,1,0:T(8,128)(2,1)S(1)}, bf16[16,256,128]{2,1,0:T(8,128)(2,1)}, u32[]{:S(2)}) copy-start(bf16[16,256,128]{2,1,0:T(8,128)(2,1)} %copy-done.10) | copy-start | bytes 3145732
  177.1 39.4 %collective-permute-start.14 = (bf16[16,256,128]{2,1,0:T(8,128)(2,1)}, bf16[16,256,128]{2,1,0:T(8,128)(2,1)S(1)}, u32[]{:S(2)}, u32[]{:S(2)}) collective-permute-start(bf16[16,256,128]{2,1,0:T(8,128)(2,1)} %collective-permute-done.13), channel_id=1, source_target_pairs={{1,0},{2,1},{3,2},{4,3},{5,4},{6,5},{7,6},{8,7},{9,8},{10,9},{11,1... | collective-permute-start | bytes 3145736 | tf_op jit(solution)/shard_map/ppermute | solution.py:39
  217.7 13.1 %copy-start.15 = (bf16[16,256,128]{2,1,0:T(8,128)(2,1)S(1)}, bf16[16,256,128]{2,1,0:T(8,128)(2,1)}, u32[]{:S(2)}) copy-start(bf16[16,256,128]{2,1,0:T(8,128)(2,1)} %custom-call.7) | copy-start | bytes 3145732
  240.5 18.6 %copy-start.2 = (bf16[64,256,128]{2,1,0:T(8,128)(2,1)S(1)}, bf16[64,256,128]{2,1,0:T(8,128)(2,1)}, u32[]{:S(2)}) copy-start(bf16[64,256,128]{2,1,0:T(8,128)(2,1)} %gather_fusion) | copy-start | bytes 12582916 | tf_op jit(solution)/shard_map/while
  276.5 18.6 %copy-start.2 = (bf16[64,256,128]{2,1,0:T(8,128)(2,1)S(1)}, bf16[64,256,128]{2,1,0:T(8,128)(2,1)}, u32[]{:S(2)}) copy-start(bf16[64,256,128]{2,1,0:T(8,128)(2,1)} %gather_fusion) | copy-start | bytes 12582916 | tf_op jit(solution)/shard_map/while
  312.5 18.6 %copy-start.2 = (bf16[64,256,128]{2,1,0:T(8,128)(2,1)S(1)}, bf16[64,256,128]{2,1,0:T(8,128)(2,1)}, u32[]{:S(2)}) copy-start(bf16[64,256,128]{2,1,0:T(8,128)(2,1)} %gather_fusion) | copy-start | bytes 12582916 | tf_op jit(solution)/shard_map/while
  348.5 18.6 %copy-start.2 = (bf16[64,256,128]{2,1,0:T(8,128)(2,1)S(1)}, bf16[64,256,128]{2,1,0:T(8,128)(2,1)}, u32[]{:S(2)}) copy-start(bf16[64,256,128]{2,1,0:T(8,128)(2,1)} %gather_fusion) | copy-start | bytes 12582916 | tf_op jit(solution)/shard_map/while
  384.5 18.6 %copy-start.2 = (bf16[64,256,128]{2,1,0:T(8,128)(2,1)S(1)}, bf16[64,256,128]{2,1,0:T(8,128)(2,1)}, u32[]{:S(2)}) copy-start(bf16[64,256,128]{2,1,0:T(8,128)(2,1)} %gather_fusion) | copy-start | bytes 12582916 | tf_op jit(solution)/shard_map/while
  420.5 18.6 %copy-start.2 = (bf16[64,256,128]{2,1,0:T(8,128)(2,1)S(1)}, bf16[64,256,128]{2,1,0:T(8,128)(2,1)}, u32[]{:S(2)}) copy-start(bf16[64,256,128]{2,1,0:T(8,128)(2,1)} %gather_fusion) | copy-start | bytes 12582916 | tf_op jit(solution)/shard_map/while
  456.5 18.6 %copy-start.2 = (bf16[64,256,128]{2,1,0:T(8,128)(2,1)S(1)}, bf16[64,256,128]{2,1,0:T(8,128)(2,1)}, u32[]{:S(2)}) copy-start(bf16[64,256,128]{2,1,0:T(8,128)(2,1)} %gather_fusion) | copy-start | bytes 12582916 | tf_op jit(solution)/shard_map/while
  492.5 18.6 %copy-start.2 = (bf16[64,256,128]{2,1,0:T(8,128)(2,1)S(1)}, bf16[64,256,128]{2,1,0:T(8,128)(2,1)}, u32[]{:S(2)}) copy-start(bf16[64,256,128]{2,1,0:T(8,128)(2,1)} %gather_fusion) | copy-start | bytes 12582916 | tf_op jit(solution)/shard_map/while
  528.4 18.6 %copy-start.2 = (bf16[64,256,128]{2,1,0:T(8,128)(2,1)S(1)}, bf16[64,256,128]{2,1,0:T(8,128)(2,1)}, u32[]{:S(2)}) copy-start(bf16[64,256,128]{2,1,0:T(8,128)(2,1)} %gather_fusion) | copy-start | bytes 12582916 | tf_op jit(solution)/shard_map/while
  564.4 18.6 %copy-start.2 = (bf16[64,256,128]{2,1,0:T(8,128)(2,1)S(1)}, bf16[64,256,128]{2,1,0:T(8,128)(2,1)}, u32[]{:S(2)}) copy-start(bf16[64,256,128]{2,1,0:T(8,128)(2,1)} %gather_fusion) | copy-start | bytes 12582916 | tf_op jit(solution)/shard_map/while
  600.4 18.6 %copy-start.2 = (bf16[64,256,128]{2,1,0:T(8,128)(2,1)S(1)}, bf16[64,256,128]{2,1,0:T(8,128)(2,1)}, u32[]{:S(2)}) copy-start(bf16[64,256,128]{2,1,0:T(8,128)(2,1)} %gather_fusion) | copy-start | bytes 12582916 | tf_op jit(solution)/shard_map/while
  636.4 18.6 %copy-start.2 = (bf16[64,256,128]{2,1,0:T(8,128)(2,1)S(1)}, bf16[64,256,128]{2,1,0:T(8,128)(2,1)}, u32[]{:S(2)}) copy-start(bf16[64,256,128]{2,1,0:T(8,128)(2,1)} %gather_fusion) | copy-start | bytes 12582916 | tf_op jit(solution)/shard_map/while
  672.4 18.6 %copy-start.2 = (bf16[64,256,128]{2,1,0:T(8,128)(2,1)S(1)}, bf16[64,256,128]{2,1,0:T(8,128)(2,1)}, u32[]{:S(2)}) copy-start(bf16[64,256,128]{2,1,0:T(8,128)(2,1)} %gather_fusion) | copy-start | bytes 12582916 | tf_op jit(solution)/shard_map/while
  708.4 18.6 %copy-start.2 = (bf16[64,256,128]{2,1,0:T(8,128)(2,1)S(1)}, bf16[64,256,128]{2,1,0:T(8,128)(2,1)}, u32[]{:S(2)}) copy-start(bf16[64,256,128]{2,1,0:T(8,128)(2,1)} %gather_fusion) | copy-start | bytes 12582916 | tf_op jit(solution)/shard_map/while
  744.4 18.6 %copy-start.2 = (bf16[64,256,128]{2,1,0:T(8,128)(2,1)S(1)}, bf16[64,256,128]{2,1,0:T(8,128)(2,1)}, u32[]{:S(2)}) copy-start(bf16[64,256,128]{2,1,0:T(8,128)(2,1)} %gather_fusion) | copy-start | bytes 12582916 | tf_op jit(solution)/shard_map/while
  780.4 18.6 %copy-start.2 = (bf16[64,256,128]{2,1,0:T(8,128)(2,1)S(1)}, bf16[64,256,128]{2,1,0:T(8,128)(2,1)}, u32[]{:S(2)}) copy-start(bf16[64,256,128]{2,1,0:T(8,128)(2,1)} %gather_fusion) | copy-start | bytes 12582916 | tf_op jit(solution)/shard_map/while
  806.6 1.0 copy-start.16
  807.6 0.7 copy-start.1
